TPU v7x, 1024 devices: a whole 4x8x16 slice. The times are simulated.
1024 devices in a mesh: ctx: 32 (over x_lo, z), dp: 32 (over y, x_hi, core).
Axes of the slice: x: 4 (x_hi: 2, x_lo: 2; x = x_hi * 2 + x_lo), y: 8, z: 16, core: 2. Of those that a mesh axis runs over, the one named last changes fastest.
Arguments:
- query: bfloat16 [32, 4096, 1024], P('dp', 'ctx'), may hold values from -6 to 6
- key_in: bfloat16 [32, 4096, 1024], P('dp', 'ctx'), may hold values from -6 to 6
- value: bfloat16 [32, 4096, 1024], P('dp', 'ctx'), may hold values from -6 to 6
- cotangent: bfloat16 [32, 4096, 1024], P('dp', 'ctx'), may hold values from -6 to 6
- filters: bfloat16 [32, 4096], P('ctx'), may hold values from -0.09375 to 0.09375
Outputs:
- output: bfloat16 [32, 4096, 1024], P('dp', 'ctx')
- grad_query: bfloat16 [32, 4096, 1024], P('dp', 'ctx')
- grad_key: bfloat16 [32, 4096, 1024], P('dp', 'ctx')
- grad_value: bfloat16 [32, 4096, 1024], P('dp', 'ctx')
- grad_filter: float32 [32, 4096], P('ctx', 'dp')
All inputs are finite; a program needn't handle non-finite values.
Results may differ from a plain program's by a relative error of at most 0.0058.
Values may be sent and summed in bfloat16 or wider, within the bound.
No kernel may reach another device: no remote copies, remote signals or barrier semaphores. Data moves between devices by JAX's collectives and lax.ppermute only.
A program may use at most 64 MiB of HBM per device.

v0:
```python
import math

import jax
import jax.numpy as jnp
from jax import lax
from jax.sharding import PartitionSpec as P

CPG = 32
BLK = 256


def group_rows(items):
    count, width, length = items.shape
    groups = width // CPG
    return (
        items.reshape(count, groups, CPG, length)
        .transpose(1, 0, 2, 3)
        .reshape(groups, count * CPG, length)
    )


def ungroup_rows(rows, count):
    groups, columns, length = rows.shape
    return (
        rows.reshape(groups, count, CPG, length)
        .transpose(1, 0, 2, 3)
        .reshape(count, groups * CPG, length)
    )


def band_blocks(filters_local, blocksize):
    groups, length = filters_local.shape
    width = length + blocksize
    extended = jnp.concatenate(
        [filters_local, jnp.zeros((groups, blocksize), filters_local.dtype)], axis=1
    )
    tiled = jnp.tile(extended, (1, blocksize))[:, : blocksize * (width - 1)]
    shifted = tiled.reshape(groups, blocksize, width - 1)[:, :, :length]
    nblocks = length // blocksize
    return shifted.reshape(groups, blocksize, nblocks, blocksize).transpose(0, 2, 1, 3)


def earlier_blocks(rows, blocksize):
    groups, columns, length = rows.shape
    nblocks = length // blocksize
    blocks = rows.reshape(groups, columns, nblocks, blocksize)
    padded = jnp.concatenate(
        [jnp.zeros((groups, columns, nblocks - 1, blocksize), rows.dtype), blocks], axis=2
    )
    return jnp.stack(
        [
            padded[:, :, nblocks - 1 - offset : 2 * nblocks - 1 - offset]
            for offset in range(nblocks)
        ],
        axis=3,
    )


def later_blocks(rows, blocksize):
    groups, columns, length = rows.shape
    nblocks = length // blocksize
    blocks = rows.reshape(groups, columns, nblocks, blocksize)
    padded = jnp.concatenate(
        [blocks, jnp.zeros((groups, columns, nblocks - 1, blocksize), rows.dtype)], axis=2
    )
    return jnp.stack([padded[:, :, offset : offset + nblocks] for offset in range(nblocks)], axis=3)


def convolve(rows, matrices, blocksize):
    earlier = earlier_blocks(rows, blocksize)
    result = jnp.einsum("gridb,gdba->gria", earlier, matrices, preferred_element_type=jnp.float32)
    return result.reshape(rows.shape)


def convolve_adjoint(rows, matrices, blocksize):
    later = later_blocks(rows, blocksize)
    result = jnp.einsum("grjda,gdba->grjb", later, matrices, preferred_element_type=jnp.float32)
    return result.reshape(rows.shape)


def filter_lags(grad_rows, mixed_rows, blocksize):
    groups, columns, length = grad_rows.shape
    nblocks = length // blocksize
    reversed_grads = grad_rows.reshape(groups, columns, nblocks, blocksize)[:, :, :, ::-1]
    earlier = earlier_blocks(mixed_rows, blocksize)
    square = jnp.einsum(
        "gria,gridb->gdab", reversed_grads, earlier, preferred_element_type=jnp.float32
    )
    padded = jnp.concatenate([square, jnp.zeros_like(square)], axis=3)
    padded = padded.reshape(groups, nblocks, 2 * blocksize * blocksize)[
        :, :, : blocksize * (2 * blocksize - 1)
    ]
    diagonal = padded.reshape(groups, nblocks, blocksize, 2 * blocksize - 1).sum(axis=2)
    extended = jnp.concatenate([diagonal, jnp.zeros((groups, nblocks, 1), jnp.float32)], axis=2)
    nearer = extended[:, :, :blocksize][:, :, ::-1]
    farther = extended[:, :, blocksize:][:, :, ::-1]
    farther = jnp.concatenate(
        [farther[:, 1:], jnp.zeros((groups, 1, blocksize), jnp.float32)], axis=1
    )
    return (nearer + farther).reshape(groups, length)


def local(query, key_in, value, cotangent, filters):
    seqcount = query.shape[0]
    mixed = (key_in.astype(jnp.float32) * value.astype(jnp.float32)).astype(jnp.bfloat16)
    gradin = (cotangent.astype(jnp.float32) * query.astype(jnp.float32)).astype(jnp.bfloat16)
    mixed_cols = mixed.transpose(0, 2, 1)
    gradin_cols = gradin.transpose(0, 2, 1)
    matrices = band_blocks(filters, BLK)
    items = lax.all_to_all(mixed_cols, "ctx", split_axis=1, concat_axis=2, tiled=True)
    conv_items = convolve(group_rows(items), matrices, BLK).astype(jnp.bfloat16)
    conv_own = ungroup_rows(conv_items, items.shape[0])
    conv_cols = lax.all_to_all(conv_own, "ctx", split_axis=2, concat_axis=1, tiled=True)
    grad_own = lax.all_to_all(gradin_cols, "ctx", split_axis=1, concat_axis=2, tiled=True)
    grad_rows = group_rows(grad_own)
    adjoint_own = ungroup_rows(
        convolve_adjoint(grad_rows, matrices, BLK).astype(jnp.bfloat16), seqcount
    )
    adjoint_cols = lax.all_to_all(adjoint_own, "ctx", split_axis=2, concat_axis=1, tiled=True)
    lag_sums = filter_lags(grad_rows, group_rows(items), BLK)
    conv = conv_cols.transpose(0, 2, 1)
    adjoint = adjoint_cols.transpose(0, 2, 1)
    output = (query.astype(jnp.float32) * conv.astype(jnp.float32)).astype(jnp.bfloat16)
    grad_query = (cotangent.astype(jnp.float32) * conv.astype(jnp.float32)).astype(jnp.bfloat16)
    grad_key = (adjoint.astype(jnp.float32) * value.astype(jnp.float32)).astype(jnp.bfloat16)
    grad_value = (adjoint.astype(jnp.float32) * key_in.astype(jnp.float32)).astype(jnp.bfloat16)
    total_length = query.shape[1] * lax.axis_size("ctx")
    total_batch = seqcount * lax.axis_size("dp")
    scale_factor = 1.0 / math.sqrt(total_batch * total_length * CPG)
    grad_filter = lax.psum_scatter(
        lag_sums * jnp.float32(scale_factor), "dp", scatter_dimension=1, tiled=True
    )
    return (output, grad_query, grad_key, grad_value, grad_filter)


def solution(mesh):
    placed = (
        P("dp", "ctx", None),
        P("dp", "ctx", None),
        P("dp", "ctx", None),
        P("dp", "ctx", None),
        P("ctx", None),
    )
    return jax.shard_map(
        local,
        mesh=mesh,
        in_specs=placed,
        out_specs=(
            P("dp", "ctx", None),
            P("dp", "ctx", None),
            P("dp", "ctx", None),
            P("dp", "ctx", None),
            P("ctx", "dp"),
        ),
        check_vma=False,
    )
```

profile of v0, /device:TPU:16, one launch (start us, length us, event | category | flops | bytes accessed | tf_op | source)
XLA Modules:
  0.0 436.5 jit_solution(1717287985701808012)
XLA Ops:
  13.5 20.6 %all-to-all-start.2 = ((bf16[32,2,2048]{2,1,0:T(2,128)(2,1)}), bf16[32,2,2048]{2,1,0:T(2,128)(2,1)S(1)}, u32[]{:S(2)}, u32[]{:S(2)}) async-start(bf16[32,2,2048]{2,1,0:T(2,128)(2,1)} %reshape.128), calls=%async_computation.2 | async-start | bytes 524288 | tf_op jit(solution)/shard_map/all_to_all | solution.py:114
  34.4 3.4 copy.296
  37.8 43.4 %slice_reduce_fusion = bf16[1113856]{0:T(1024)(128)(2,1)S(1)} fusion(bf16[1,1114112]{1,0:T(2,128)(2,1)S(1)} %bitcast.305), kind=kLoop, calls=%fused_computation | loop fusion | bytes 4455424 | tf_op jit(solution)/shard_map/slice | solution.py:37
  81.2 5.1 %reshape.104 = bf16[1,256,4351]{2,1,0:T(8,128)(2,1)} reshape(bf16[1113856]{0:T(1024)(128)(2,1)S(1)} %slice_reduce_fusion) | data formatting | bytes 4455424 | tf_op jit(solution)/shard_map/reshape | solution.py:38
  87.9 2.5 copy.257
  90.3 2.8 copy.258
  96.3 2.8 copy.280
  99.1 22.6 %reduce.6 = bf16[4096,32]{1,0:T(8,128)(2,1)S(1)} reduce(bf16[4096,1,32]{2,1,0:T(2,128)(2,1)S(1)} %bitcast.310, bf16[]{:T(256)} %broadcast.29), dimensions={1}, to_apply=%bitcast.299.reduce_sub_computation | reduce | bytes 524290
  123.4 13.2 %all-to-all-start.3 = ((bf16[32,2,2048]{2,1,0:T(2,128)(2,1)}), bf16[32,2,2048]{2,1,0:T(2,128)(2,1)S(1)}, u32[]{:S(2)}, u32[]{:S(2)}) async-start(bf16[32,2,2048]{2,1,0:T(2,128)(2,1)} %reshape.130), calls=%async_computation.3 | async-start | bytes 524288 | tf_op jit(solution)/shard_map/all_to_all | solution.py:119
  138.9 19.5 %all-to-all-done.3 = bf16[32,2,2048]{2,1,0:T(2,128)(2,1)S(1)} async-done(((bf16[32,2,2048]{2,1,0:T(2,128)(2,1)}), bf16[32,2,2048]{2,1,0:T(2,128)(2,1)S(1)}, u32[]{:S(2)}, u32[]{:S(2)}) %all-to-all-start.3) | async-done | bytes 262176 | tf_op jit(solution)/shard_map/all_to_all | solution.py:119
  163.5 2.2 reduce.7
  166.5 4.3 all-to-all-start
  171.1 20.7 %all-to-all-done = bf16[32,2,2048]{2,1,0:T(2,128)(2,1)S(1)} async-done(((bf16[32,2,2048]{2,1,0:T(2,128)(2,1)}), bf16[32,2,2048]{2,1,0:T(2,128)(2,1)S(1)}, u32[]{:S(2)}, u32[]{:S(2)}) %all-to-all-start) | async-done | bytes 262176 | tf_op jit(solution)/shard_map/all_to_all | solution.py:110
  195.3 3.3 fusion.6
  198.5 5.4 %copy.295 = f32[1,16,256,256]{3,2,1,0:T(8,128)} copy(f32[1,16,256,256]{2,3,1,0:T(8,128)} %fusion.6) | data formatting | bytes 8388608
  203.9 6.6 %concatenate.22.clone = f32[1,16,256,512]{3,2,1,0:T(8,128)} pad(f32[1,16,256,256]{3,2,1,0:T(8,128)} %copy.295, f32[]{:T(128)} %constant.4.clone.1), padding=0_0x0_0x0_0x0_256 | pad | bytes 12582916 | tf_op jit(solution)/shard_map/concatenate | solution.py:89
  210.5 6.2 %reshape.109 = f32[1,16,131072]{2,1,0:T(8,128)} reshape(f32[1,16,256,512]{3,2,1,0:T(8,128)} %concatenate.22.clone) | data formatting | bytes 16777216 | tf_op jit(solution)/shard_map/reshape | solution.py:90
  216.7 7.1 %slice.163 = f32[1,16,130816]{2,1,0:T(8,128)} slice(f32[1,16,131072]{2,1,0:T(8,128)} %reshape.109), slice={[0:1], [0:16], [0:130816]} | slice | bytes 16744448 | tf_op jit(solution)/shard_map/slice | solution.py:90
  223.8 11.7 %reshape.110 = f32[16,256,511]{2,1,0:T(8,128)} reshape(f32[1,16,130816]{2,1,0:T(8,128)} %slice.163) | data formatting | bytes 16744448 | tf_op jit(solution)/shard_map/reshape | solution.py:93
  235.5 4.5 %reduce_sum.11 = f32[16,511]{1,0:T(8,128)S(1)} reduce(f32[16,256,511]{2,1,0:T(8,128)} %reshape.110, f32[]{:T(128)} %constant.4.clone.1), dimensions={1}, to_apply=%region_0.0 | reduce | flops 2084880 | bytes 8404932 | tf_op jit(solution)/shard_map/reduce_sum | solution.py:93
  240.2 2.8 copy.259
  242.9 22.6 %reduce.8 = bf16[4096,32]{1,0:T(8,128)(2,1)S(1)} reduce(bf16[4096,1,32]{2,1,0:T(2,128)(2,1)S(1)} %bitcast.308, bf16[]{:T(256)} %broadcast.29), dimensions={1}, to_apply=%bitcast.295.reduce_sub_computation | reduce | bytes 524290
  267.2 3.9 all-to-all-start.1
  275.4 146.9 %reduce-scatter.4.cloned.1.call-done = f32[128,1]{1,0:T(8,128)} async-done(((f32[4096,1]{1,0:T(8,128)}), f32[128,1]{1,0:T(8,128)}) %reduce-scatter.4.cloned.1.call-update) | async-done | bytes 528
  (109 shorter events, 37.7 us)
Async XLA Ops:
  7.2 27.0 %copy-start.7 = (bf16[1,4096]{1,0:T(2,128)(2,1)S(1)}, bf16[1,4096]{1,0:T(2,128)(2,1)}, u32[]{:S(2)}) copy-start(bf16[1,4096]{1,0:T(2,128)(2,1)} %param.9) | copy-start | bytes 24580
  8.3 25.8 %copy-start = (bf16[1,128,1024]{1,2,0:T(8,128)(2,1)}, bf16[1,128,1024]{1,2,0:T(8,128)(2,1)S(1)}, u32[]{:S(2)}) copy-start(bf16[1,128,1024]{1,2,0:T(8,128)(2,1)S(1)} %copy.237) | copy-start | bytes 786436
  9.5 24.6 %copy-start.2 = (bf16[1,128,1024]{1,2,0:T(8,128)(2,1)}, bf16[1,128,1024]{1,2,0:T(8,128)(2,1)S(1)}, u32[]{:S(2)}) copy-start(bf16[1,128,1024]{1,2,0:T(8,128)(2,1)S(1)} %copy.262) | copy-start | bytes 786436
  13.5 79.7 %all-to-all-start.2 = ((bf16[32,2,2048]{2,1,0:T(2,128)(2,1)}), bf16[32,2,2048]{2,1,0:T(2,128)(2,1)S(1)}, u32[]{:S(2)}, u32[]{:S(2)}) async-start(bf16[32,2,2048]{2,1,0:T(2,128)(2,1)} %reshape.128), calls=%async_computation.2 | async-start | bytes 524288 | tf_op jit(solution)/shard_map/all_to_all | solution.py:114
  86.3 1.6 slice-start
  93.2 1.7 copy-start.4
  123.4 35.0 %all-to-all-start.3 = ((bf16[32,2,2048]{2,1,0:T(2,128)(2,1)}), bf16[32,2,2048]{2,1,0:T(2,128)(2,1)S(1)}, u32[]{:S(2)}, u32[]{:S(2)}) async-start(bf16[32,2,2048]{2,1,0:T(2,128)(2,1)} %reshape.130), calls=%async_computation.3 | async-start | bytes 524288 | tf_op jit(solution)/shard_map/all_to_all | solution.py:119
  166.5 25.3 %all-to-all-start = ((bf16[32,2,2048]{2,1,0:T(2,128)(2,1)}), bf16[32,2,2048]{2,1,0:T(2,128)(2,1)S(1)}, u32[]{:S(2)}, u32[]{:S(2)}) async-start(bf16[32,2,2048]{2,1,0:T(2,128)(2,1)} %reshape.124), calls=%async_computation | async-start | bytes 524288 | tf_op jit(solution)/shard_map/all_to_all | solution.py:110
  192.4 1.6 copy-start.5
  267.2 156.5 %all-to-all-start.1 = ((bf16[32,2,2048]{2,1,0:T(2,128)(2,1)}), bf16[32,2,2048]{2,1,0:T(2,128)(2,1)S(1)}, u32[]{:S(2)}, u32[]{:S(2)}) async-start(bf16[32,2,2048]{2,1,0:T(2,128)(2,1)} %reshape.126), calls=%async_computation.1 | async-start | bytes 524288 | tf_op jit(solution)/shard_map/all_to_all | solution.py:113
  271.1 151.2 %reduce-scatter.4.cloned.1.call-start = ((), (), s32[]{:S(2)}) async-start(), calls=%async_computation.5 | async-start | bytes 2162688
  271.5 2.2 copy-start.6
  274.5 153.1 %copy-start.1 = (bf16[1,128,1024]{1,2,0:T(8,128)(2,1)S(1)}, bf16[1,128,1024]{1,2,0:T(8,128)(2,1)}, u32[]{:S(2)}) copy-start(bf16[1,128,1024]{1,2,0:T(8,128)(2,1)} %copy-done) | copy-start | bytes 786436
  274.5 153.1 %copy-start.3 = (bf16[1,128,1024]{1,2,0:T(8,128)(2,1)S(1)}, bf16[1,128,1024]{1,2,0:T(8,128)(2,1)}, u32[]{:S(2)}) copy-start(bf16[1,128,1024]{1,2,0:T(8,128)(2,1)} %copy-done.2) | copy-start | bytes 786436
Sparse Core Ops, SparseCore 0:
  277.8 144.4 reduce-scatter.3
where the time goes:
time: 440 us; the launch traced here: 436 us
  waiting for transfers between devices  187 us (42%)
  local copies, waits for them, and re-layouts  131 us (30%)
  other arithmetic  55.2 us (13%)
  starting transfers between devices  42 us (10%)
  between operations  15 us (3%)
  matrix products  5.78 us (1%)
    unnamed x2, waiting for transfers between devices  147 us
    unnamed x7, other arithmetic  49.7 us
    slice x1, local copies, waits for them, and re-layouts, band_blocks(): tiled = jnp.tile(extended, (1, blocksize))[:, :blocksize * (width - 1)]  43.4 us
    unnamed x74, local copies, waits for them, and re-layouts  31.8 us
    all_to_all x1, waiting for transfers between devices, local(): lax.all_to_all(mixed_cols, 'ctx', split_axis=1, concat_axis=2, tiled=True)  20.7 us
    all_to_all x1, starting transfers between devices, local(): lax.all_to_all(gradin_cols, 'ctx', split_axis=1, concat_axis=2, tiled=True)  20.6 us
    all_to_all x1, waiting for transfers between devices, local(): lax.all_to_all(adjoint_own, 'ctx', split_axis=2, concat_axis=1, tiled=True)  19.5 us
    all_to_all x1, starting transfers between devices, local(): lax.all_to_all(adjoint_own, 'ctx', split_axis=2, concat_axis=1, tiled=True)  13.2 us
  transfers between devices with their start and end apart: 5, of which 3 were waited for; matrix products, arithmetic and copies ran while one was open for 15% of the time, Pallas kernels for 0%

commit v1 on v0

v1 whole, which is shorter than its diff:
```python
import math

import jax
import jax.numpy as jnp
from jax import lax
from jax.experimental import pallas as pl
from jax.experimental.pallas import tpu as pltpu
from jax.sharding import PartitionSpec as P


CPG = 32
BLK = 256
VMEM = pl.BlockSpec(memory_space=pltpu.VMEM)
F32 = jnp.float32
BF16 = jnp.bfloat16


ANY = pl.BlockSpec(memory_space=pl.ANY)
DMA = pltpu.SemaphoreType.DMA
PARTS = 4


def call(kernel, out_shape, flops, moved, outs=VMEM, limit=16, **kw):
    return pl.pallas_call(
        kernel,
        out_shape=out_shape,
        out_specs=jax.tree.map(lambda _: outs, out_shape),
        cost_estimate=pl.CostEstimate(flops=flops, bytes_accessed=moved, transcendentals=0),
        compiler_params=pltpu.CompilerParams(vmem_limit_bytes=limit * 2**20),
        **kw,
    )


def gate_kernel(k_ref, v_ref, q_ref, g_ref, out_ref, wide_ref, held_ref, in_sem, out_sem):
    groups, _, pos = out_ref.shape
    step = groups // PARTS
    span = step * CPG
    pairs = ((k_ref, v_ref), (g_ref, q_ref))
    loads = []
    for part in range(PARTS):
        at = pl.ds(part * span, span)
        row = [
            [
                pltpu.make_async_copy(
                    ref.at[:, at], wide_ref.at[2 * h + j, :, at], in_sem.at[part, 2 * h + j]
                )
                for j, ref in enumerate(pair)
            ]
            for h, pair in enumerate(pairs)
        ]
        for pair in row:
            for copy in pair:
                copy.start()
        loads.append(row)
    stores = []
    for part in range(PARTS):
        mine = pl.ds(part * step, step)
        for h in range(2):
            for copy in loads[part][h]:
                copy.wait()
            at = slice(part * span, (part + 1) * span)
            one = wide_ref[2 * h, :, at].astype(F32) * wide_ref[2 * h + 1, :, at].astype(F32)
            rows = one.astype(BF16).T.reshape(step, CPG, pos)
            held_ref[part * step : (part + 1) * step, h * CPG : (h + 1) * CPG, :] = rows
        copy = pltpu.make_async_copy(held_ref.at[mine], out_ref.at[mine], out_sem.at[part])
        copy.start()
        stores.append(copy)
    for copy in stores:
        copy.wait()


def band_kernel(f_ref, e_ref):
    length = f_ref.shape[1]
    filt = f_ref[...].astype(F32)
    ext = jnp.concatenate([jnp.zeros((1, BLK), F32), filt], axis=1)
    width = length + BLK
    wide = jnp.broadcast_to(ext, (8, width))
    row = lax.broadcasted_iota(jnp.int32, (8, width), 0)
    base = wide
    for r in range(1, 8):
        base = jnp.where(row == r, pltpu.roll(wide, r, 1), base)
    prev = None
    for q in range(16):
        cur = base if q == 0 else pltpu.roll(base, 8 * q, 1)
        if q % 2 == 0:
            prev = cur
            continue
        pair = jnp.concatenate([prev, cur], axis=0).astype(BF16)
        at = 8 * (q - 1)
        e_ref[at : at + 16, :] = pair[:, BLK:]
        e_ref[128 + at : 128 + at + 16, :] = pair[:, 128 : 128 + length]


def rows_of(ref, half):
    pieces = ref.shape[0]
    part = ref[:, half * CPG : (half + 1) * CPG, :]
    pair = part.reshape(pieces // 2, 2, CPG, 128)
    return jnp.concatenate([pair[:, 0], pair[:, 1]], axis=-1).reshape(pieces // 2 * CPG, BLK)


def put_rows(ref, half, rows):
    pieces = ref.shape[0]
    blocks = rows.reshape(pieces // 2, CPG, BLK)
    both = jnp.stack([blocks[:, :, :128], blocks[:, :, 128:]], axis=1)
    ref[:, half * CPG : (half + 1) * CPG, :] = both.reshape(pieces, CPG, 128)


def conv_kernel(in_ref, e_ref, out_ref, held_ref, x_ref, acc_ref, sem):
    nblocks = in_ref.shape[0] // 2
    x_ref[...] = rows_of(in_ref, 0)
    for d in range(nblocks):
        n = (nblocks - d) * CPG
        part = jnp.dot(
            x_ref[:n, :], e_ref[:, d * BLK : (d + 1) * BLK], preferred_element_type=F32
        )
        if d == 0:
            acc_ref[...] = part
        else:
            acc_ref[d * CPG :, :] += part
    put_rows(held_ref, 0, acc_ref[...].astype(BF16))
    half = pl.ds(0, CPG)
    first = pltpu.make_async_copy(held_ref.at[:, half, :], out_ref.at[:, half, :], sem.at[0])
    first.start()
    x_ref[...] = rows_of(in_ref, 1)
    for d in range(nblocks):
        n = (nblocks - d) * CPG
        part = lax.dot_general(
            x_ref[d * CPG :, :],
            e_ref[:, d * BLK : (d + 1) * BLK],
            (((1,), (1,)), ((), ())),
            preferred_element_type=F32,
        )
        if d == 0:
            acc_ref[...] = part
        else:
            acc_ref[:n, :] += part
    put_rows(held_ref, 1, acc_ref[...].astype(BF16))
    half = pl.ds(CPG, CPG)
    second = pltpu.make_async_copy(held_ref.at[:, half, :], out_ref.at[:, half, :], sem.at[1])
    second.start()
    first.wait()
    second.wait()


def lag_kernel(scale, in_ref, out_ref, xt_ref, g_ref, s_ref):
    nblocks = in_ref.shape[0] // 2
    total = nblocks * CPG
    length = nblocks * BLK
    xt_ref[...] = rows_of(in_ref, 0).T
    g_ref[:total, :] = rows_of(in_ref, 1)
    g_ref[total:, :] = jnp.zeros((128, BLK), BF16)
    s_ref[:, length:] = jnp.zeros((BLK, 128), F32)
    for d in range(nblocks):
        n = -(-(total - d * CPG) // 128) * 128
        s_ref[:, d * BLK : (d + 1) * BLK] = jnp.dot(
            xt_ref[:, :n], g_ref[d * CPG : d * CPG + n, :], preferred_element_type=F32
        )
    width = length + 128
    zeros = jnp.zeros((8, 128), F32)
    acc = None
    for q in range(15, -1, -1):
        low = s_ref[8 * q : 8 * q + 8, :length]
        high = s_ref[128 + 8 * q : 128 + 8 * q + 8, 128:]
        term = jnp.concatenate([low + high, zeros], axis=1)
        acc = term if acc is None else pltpu.roll(acc, width - 8, 1) + term
    row = lax.broadcasted_iota(jnp.int32, (8, width), 0)
    lined = acc
    for r in range(1, 8):
        lined = jnp.where(row == r, pltpu.roll(acc, width - r, 1), lined)
    sums = jnp.sum(lined, axis=0, keepdims=True) * scale
    for i in range(length // 128):
        out_ref[i] = sums[:, 128 * i : 128 * (i + 1)]


def close_kernel(
    in_ref, k_ref, v_ref, q_ref, g_ref, out_ref, gq_ref, gk_ref, gv_ref, held_ref, sem
):
    groups, _, pos = in_ref.shape
    step = groups // PARTS
    span = step * CPG
    copies = []
    for part in range(PARTS):
        at = slice(part * span, (part + 1) * span)
        for h, gates, outs in ((0, (q_ref, g_ref), (out_ref, gq_ref)), (1, (v_ref, k_ref), (gk_ref, gv_ref))):
            rows = in_ref[part * step : (part + 1) * step, h * CPG : (h + 1) * CPG, :]
            wide = rows.reshape(span, pos).T.astype(F32)
            for j in range(2):
                i = 2 * h + j
                held_ref[i, :, at] = (gates[j][:, at].astype(F32) * wide).astype(BF16)
                into = outs[j].at[:, pl.ds(part * span, span)]
                copy = pltpu.make_async_copy(
                    held_ref.at[i, :, pl.ds(part * span, span)], into, sem.at[part, i]
                )
                copy.start()
                copies.append(copy)
    for copy in copies:
        copy.wait()


def halve(terms, replicas):
    me = lax.axis_index("dp")
    bit = replicas // 2
    while bit:
        both = terms.reshape(2, bit, 1, 128)
        high = (me & bit) != 0
        kept = jnp.where(high, both[1], both[0])
        away = jnp.where(high, both[0], both[1])
        got = lax.ppermute(away, "dp", [(i, i ^ bit) for i in range(replicas)])
        terms = kept + got
        bit //= 2
    return terms.reshape(1, 128)


def step(query, key_in, value, cotangent, filters):
    seqcount, pos, channels = query.shape
    groups = channels // CPG
    pieces = lax.axis_size("ctx")
    replicas = lax.axis_size("dp")
    length = pos * pieces
    nblocks = length // BLK
    flat = [a.reshape(pos, channels) for a in (key_in, value, query, cotangent)]
    held = jax.ShapeDtypeStruct((groups, 2 * CPG, pos), BF16)
    size = groups * 2 * CPG * pos * 2
    sent = call(
        gate_kernel,
        held,
        2 * pos * channels,
        3 * size,
        ANY,
        56,
        in_specs=[ANY] * 4,
        scratch_shapes=[
            pltpu.VMEM((4, pos, channels), BF16),
            pltpu.VMEM(held.shape, BF16),
            DMA((PARTS, 4)),
            DMA((PARTS,)),
        ],
        name="gate",
    )(*flat)
    band = call(
        band_kernel,
        jax.ShapeDtypeStruct((BLK, length), BF16),
        BLK * length * 2,
        BLK * length * 2,
        in_specs=[VMEM],
        name="band",
    )(filters)
    owned = lax.all_to_all(sent, "ctx", split_axis=0, concat_axis=0, tiled=True)
    work = 2 * CPG * length * length
    result = call(
        conv_kernel,
        held,
        2 * work,
        2 * size + BLK * length * 2,
        ANY,
        in_specs=[VMEM] * 2,
        scratch_shapes=[
            pltpu.VMEM(held.shape, BF16),
            pltpu.VMEM((nblocks * CPG, BLK), BF16),
            pltpu.VMEM((nblocks * CPG, BLK), F32),
            DMA((2,)),
        ],
        name="conv",
    )(owned, band)
    owned, result = lax.optimization_barrier((owned, result))
    back = lax.all_to_all(result, "ctx", split_axis=0, concat_axis=0, tiled=True)
    scale = 1.0 / math.sqrt(seqcount * replicas * length * CPG)

    def lag_body(*refs):
        lag_kernel(scale, *refs)

    lags_of = call(
        lag_body,
        jax.ShapeDtypeStruct((length // 128, 1, 128), F32),
        work,
        size + BLK * length * 8,
        in_specs=[VMEM],
        scratch_shapes=[
            pltpu.VMEM((BLK, nblocks * CPG), BF16),
            pltpu.VMEM((nblocks * CPG + 128, BLK), BF16),
            pltpu.VMEM((BLK, length + 128), F32),
        ],
        name="lags",
    )
    lags = lags_of(owned)
    grad_filter = halve(lags, replicas)
    wide = jax.ShapeDtypeStruct((pos, channels), BF16)
    outs = call(
        close_kernel,
        (wide,) * 4,
        4 * pos * channels,
        5 * size,
        ANY,
        in_specs=[VMEM] * 5,
        scratch_shapes=[pltpu.VMEM((4, pos, channels), BF16), DMA((PARTS, 4))],
        name="close",
    )(back, *flat)
    return tuple(o.reshape(seqcount, pos, channels) for o in outs) + (grad_filter,)


def solution(mesh):
    spread = P("dp", "ctx", None)
    return jax.shard_map(
        step,
        mesh=mesh,
        in_specs=(spread,) * 4 + (P("ctx", None),),
        out_specs=(spread,) * 4 + (P("ctx", "dp"),),
        check_vma=False,
    )
```

time: 440 us -> 105 us (0.24)
  the two profiles are of different devices: /device:TPU:16 before, /device:TPU:64 now
where the time goes in v1:
time: 105 us; the launch traced here: 104 us
  waiting for transfers between devices  51.2 us (49%)
  starting transfers between devices  43.3 us (41%)
  Pallas kernels  8.52 us (8%)
    all_to_all x1, waiting for transfers between devices, step(): owned = lax.all_to_all(sent, 'ctx', split_axis=0, concat_axis=0, tiled=True)  31.6 us
    ppermute x5, starting transfers between devices, halve(): got = lax.ppermute(away, 'dp', [(i, i ^ bit) for i in range(replicas)])  19.6 us
    all_to_all x1, starting transfers between devices, step(): owned = lax.all_to_all(sent, 'ctx', split_axis=0, concat_axis=0, tiled=True)  19.5 us
    ppermute x5, waiting for transfers between devices, halve(): got = lax.ppermute(away, 'dp', [(i, i ^ bit) for i in range(replicas)])  10 us
    all_to_all x1, waiting for transfers between devices, step(): lax.all_to_all(result, 'ctx', split_axis=0, concat_axis=0, tiled=True)  9.56 us
    all_to_all x1, starting transfers between devices, step(): lax.all_to_all(result, 'ctx', split_axis=0, concat_axis=0, tiled=True)  4.22 us
    pallas_call x1, Pallas kernels, step(): call(gate_kernel, held, 2 * pos * channels, 3 * size, ANY, 56, in_specs=[...  2.32 us
    pallas_call x1, Pallas kernels, step(): lags = lags_of(owned)  2.26 us
  transfers between devices with their start and end apart: 7, of which 6 were waited for; matrix products, arithmetic and copies ran while one was open for 1% of the time, Pallas kernels for 1%

profile of v1, /device:TPU:64, one launch (start us, length us, event | category | flops | bytes accessed | tf_op | source)
XLA Modules:
  0.0 104.5 jit_solution(268517734803403731)
XLA Ops:
  0.6 2.3 %gate.1 = bf16[32,64,128]{2,1,0:T(8,128)(2,1)} custom-call(bf16[128,1024]{1,0:T(8,128)(2,1)} %bitcast.10, bf16[128,1024]{1,0:T(8,128)(2,1)} %bitcast.12, bf16[128,1024]{1,0:T(8,128)(2,1)} %bitcast.14, bf16[128,1024]{1,0:T(8,128)(2,1)} %bitcast.16), custom_call_target="tpu_custom_call" | custom-call | flops 262144 | bytes 1572864 | tf_op jit(solution)/shard_map/gate/pallas_call | solution.py:224
  3.0 19.5 %all-to-all-start = ((bf16[32,64,128]{2,1,0:T(8,128)(2,1)}), bf16[32,64,128]{2,1,0:T(8,128)(2,1)S(1)}, u32[]{:S(2)}, u32[]{:S(2)}) async-start(bf16[32,64,128]{2,1,0:T(8,128)(2,1)} %gate.1), calls=%async_computation | async-start | bytes 1048576 | tf_op jit(solution)/shard_map/all_to_all | solution.py:248
  22.5 0.5 band.1.e_ref
  23.0 31.6 %all-to-all-done.in_ref.refs_0_ = bf16[32,64,128]{2,1,0:T(8,128)(2,1)S(1)} async-done(((bf16[32,64,128]{2,1,0:T(8,128)(2,1)}), bf16[32,64,128]{2,1,0:T(8,128)(2,1)S(1)}, u32[]{:S(2)}, u32[]{:S(2)}) %all-to-all-start) | async-done | bytes 524320 | tf_op jit(solution)/shard_map/all_to_all | solution.py:248
  54.7 2.2 %conv.1 = bf16[32,64,128]{2,1,0:T(8,128)(2,1)} custom-call(bf16[32,64,128]{2,1,0:T(8,128)(2,1)S(1)} %all-to-all-done.in_ref.refs_0_, bf16[256,4096]{1,0:T(8,128)(2,1)S(1)} %band.1.e_ref), custom_call_target="tpu_custom_call" | custom-call | flops 2147483648 | bytes 3145728 | tf_op jit(solution)/shard_map/conv/pallas_call | solution.py:250
  56.9 0.0 copy-start
  56.9 0.0 copy-start.1
  56.9 0.0 copy-start.2
  57.0 0.0 copy-start.3
  57.0 2.3 %lags.1 = f32[32,1,128]{2,1,0:T(1,128)S(1)} custom-call(bf16[32,64,128]{2,1,0:T(8,128)(2,1)S(1)} %all-to-all-done.in_ref.refs_0_), custom_call_target="tpu_custom_call" | custom-call | flops 1073741824 | bytes 8912896 | tf_op jit(solution)/shard_map/lags/pallas_call | solution.py:285
  59.2 7.7 %collective-permute-start = (f32[16,1,128]{2,1,0:T(1,128)S(1)}, f32[16,1,128]{2,1,0:T(1,128)S(1)}, u32[]{:S(2)}, u32[]{:S(2)}) collective-permute-start(f32[16,1,128]{2,1,0:T(1,128)S(1)} %broadcast_select_fusion), channel_id=1, source_target_pairs={{0,16},{1,17},{2,18},{3,19},{4,20},{5,21},{6,22},{7,23},{8,24},{9,... | collective-permute-start | bytes 24584 | tf_op jit(solution)/shard_map/ppermute | solution.py:208
  67.0 4.2 %all-to-all-start.1 = ((bf16[32,64,128]{2,1,0:T(8,128)(2,1)}), bf16[32,64,128]{2,1,0:T(8,128)(2,1)S(1)}, u32[]{:S(2)}, u32[]{:S(2)}) async-start(bf16[32,64,128]{2,1,0:T(8,128)(2,1)} %conv.1), calls=%async_computation.1 | async-start | bytes 1048576 | tf_op jit(solution)/shard_map/all_to_all | solution.py:266
  71.2 0.0 collective-permute-done
  71.3 2.7 %collective-permute-start.1 = (f32[8,1,128]{2,1,0:T(1,128)S(1)}, f32[8,1,128]{2,1,0:T(1,128)S(1)}, u32[]{:S(2)}, u32[]{:S(2)}) collective-permute-start(f32[8,1,128]{2,1,0:T(1,128)S(1)} %broadcast_select_fusion.2), channel_id=1, source_target_pairs={{0,8},{1,9},{2,10},{3,11},{4,12},{5,13},{6,14},{7,15},{8,0},{9,1},... | collective-permute-start | bytes 12296 | tf_op jit(solution)/shard_map/ppermute | solution.py:208
  74.0 3.7 %collective-permute-done.1 = f32[8,1,128]{2,1,0:T(1,128)S(1)} collective-permute-done((f32[8,1,128]{2,1,0:T(1,128)S(1)}, f32[8,1,128]{2,1,0:T(1,128)S(1)}, u32[]{:S(2)}, u32[]{:S(2)}) %collective-permute-start.1) | collective-permute-done | bytes 4128 | tf_op jit(solution)/shard_map/ppermute | solution.py:208
  77.7 2.6 %collective-permute-start.2 = (f32[4,1,128]{2,1,0:T(1,128)S(1)}, f32[4,1,128]{2,1,0:T(1,128)S(1)}, u32[]{:S(2)}, u32[]{:S(2)}) collective-permute-start(f32[4,1,128]{2,1,0:T(1,128)S(1)} %broadcast_select_fusion.4), channel_id=1, source_target_pairs={{0,4},{1,5},{2,6},{3,7},{4,0},{5,1},{6,2},{7,3},{8,12},{9,13},{10,... | collective-permute-start | bytes 6152 | tf_op jit(solution)/shard_map/ppermute | solution.py:208
  80.3 2.9 %collective-permute-done.2 = f32[4,1,128]{2,1,0:T(1,128)S(1)} collective-permute-done((f32[4,1,128]{2,1,0:T(1,128)S(1)}, f32[4,1,128]{2,1,0:T(1,128)S(1)}, u32[]{:S(2)}, u32[]{:S(2)}) %collective-permute-start.2) | collective-permute-done | bytes 2080 | tf_op jit(solution)/shard_map/ppermute | solution.py:208
  83.2 4.6 %collective-permute-start.3 = (f32[2,1,128]{2,1,0:T(1,128)S(1)}, f32[2,1,128]{2,1,0:T(1,128)S(1)}, u32[]{:S(2)}, u32[]{:S(2)}) collective-permute-start(f32[2,1,128]{2,1,0:T(1,128)S(1)} %broadcast_select_fusion.6), channel_id=1, source_target_pairs={{0,2},{1,3},{2,0},{3,1},{4,6},{5,7},{6,4},{7,5},{8,10},{9,11},{10,... | collective-permute-start | bytes 3080 | tf_op jit(solution)/shard_map/ppermute | solution.py:208
  87.8 2.3 %collective-permute-done.3 = f32[2,1,128]{2,1,0:T(1,128)S(1)} collective-permute-done((f32[2,1,128]{2,1,0:T(1,128)S(1)}, f32[2,1,128]{2,1,0:T(1,128)S(1)}, u32[]{:S(2)}, u32[]{:S(2)}) %collective-permute-start.3) | collective-permute-done | bytes 1056 | tf_op jit(solution)/shard_map/ppermute | solution.py:208
  90.2 1.9 %collective-permute-start.4 = (f32[1,1,128]{2,1,0:T(1,128)S(1)}, f32[1,1,128]{2,1,0:T(1,128)S(1)}, u32[]{:S(2)}, u32[]{:S(2)}) collective-permute-start(f32[1,1,128]{2,1,0:T(1,128)S(1)} %broadcast_select_fusion.8), channel_id=1, source_target_pairs={{0,1},{1,0},{2,3},{3,2},{4,5},{5,4},{6,7},{7,6},{8,9},{9,8},{10,11... | collective-permute-start | bytes 1544 | tf_op jit(solution)/shard_map/ppermute | solution.py:208
  92.1 1.1 %collective-permute-done.4 = f32[1,1,128]{2,1,0:T(1,128)S(1)} collective-permute-done((f32[1,1,128]{2,1,0:T(1,128)S(1)}, f32[1,1,128]{2,1,0:T(1,128)S(1)}, u32[]{:S(2)}, u32[]{:S(2)}) %collective-permute-start.4) | collective-permute-done | bytes 544 | tf_op jit(solution)/shard_map/ppermute | solution.py:208
  93.2 0.5 fusion.5
  93.7 9.6 %all-to-all-done.1.in_ref = bf16[32,64,128]{2,1,0:T(8,128)(2,1)S(1)} async-done(((bf16[32,64,128]{2,1,0:T(8,128)(2,1)}), bf16[32,64,128]{2,1,0:T(8,128)(2,1)S(1)}, u32[]{:S(2)}, u32[]{:S(2)}) %all-to-all-start.1) | async-done | bytes 524320 | tf_op jit(solution)/shard_map/all_to_all | solution.py:266
  103.3 1.2 %close.1 = (bf16[128,1024]{1,0:T(8,128)(2,1)}, bf16[128,1024]{1,0:T(8,128)(2,1)}, bf16[128,1024]{1,0:T(8,128)(2,1)}, bf16[128,1024]{1,0:T(8,128)(2,1)}) custom-call(bf16[32,64,128]{2,1,0:T(8,128)(2,1)S(1)} %all-to-all-done.1.in_ref, bf16[128,1024]{1,0:T(8,128)(2,1)S(1)} %bitcast.11, bf16[128,1024]{1,0:T(8,128)(2,1)S(1)} %bitcast.13, ...), custom_call_target="tpu_custom_call" | custom-call | flops 524288 | bytes 2621440 | tf_op jit(solution)/shard_map/close/pallas_call | solution.py:288
  (15 shorter events, 0.1 us)
Async XLA Ops:
  0.6 21.9 %copy-start.4 = (bf16[1,4096]{1,0:T(2,128)(2,1)S(1)}, bf16[1,4096]{1,0:T(2,128)(2,1)}, u32[]{:S(2)}) copy-start(bf16[1,4096]{1,0:T(2,128)(2,1)} %f_ref.1) | copy-start | bytes 24580
  3.0 51.7 %all-to-all-start = ((bf16[32,64,128]{2,1,0:T(8,128)(2,1)}), bf16[32,64,128]{2,1,0:T(8,128)(2,1)S(1)}, u32[]{:S(2)}, u32[]{:S(2)}) async-start(bf16[32,64,128]{2,1,0:T(8,128)(2,1)} %gate.1), calls=%async_computation | async-start | bytes 1048576 | tf_op jit(solution)/shard_map/all_to_all | solution.py:248
  56.9 46.4 %copy-start = (bf16[1,128,1024]{2,1,0:T(8,128)(2,1)S(1)}, bf16[1,128,1024]{2,1,0:T(8,128)(2,1)}, u32[]{:S(2)}) copy-start(bf16[1,128,1024]{2,1,0:T(8,128)(2,1)} %param.6) | copy-start | bytes 786436
  56.9 46.4 %copy-start.1 = (bf16[1,128,1024]{2,1,0:T(8,128)(2,1)S(1)}, bf16[1,128,1024]{2,1,0:T(8,128)(2,1)}, u32[]{:S(2)}) copy-start(bf16[1,128,1024]{2,1,0:T(8,128)(2,1)} %param.7) | copy-start | bytes 786436
  56.9 46.4 %copy-start.2 = (bf16[1,128,1024]{2,1,0:T(8,128)(2,1)S(1)}, bf16[1,128,1024]{2,1,0:T(8,128)(2,1)}, u32[]{:S(2)}) copy-start(bf16[1,128,1024]{2,1,0:T(8,128)(2,1)} %param.5) | copy-start | bytes 786436
  57.0 46.4 %copy-start.3 = (bf16[1,128,1024]{2,1,0:T(8,128)(2,1)S(1)}, bf16[1,128,1024]{2,1,0:T(8,128)(2,1)}, u32[]{:S(2)}) copy-start(bf16[1,128,1024]{2,1,0:T(8,128)(2,1)} %param.8) | copy-start | bytes 786436
  59.2 12.0 %collective-permute-start = (f32[16,1,128]{2,1,0:T(1,128)S(1)}, f32[16,1,128]{2,1,0:T(1,128)S(1)}, u32[]{:S(2)}, u32[]{:S(2)}) collective-permute-start(f32[16,1,128]{2,1,0:T(1,128)S(1)} %broadcast_select_fusion), channel_id=1, source_target_pairs={{0,16},{1,17},{2,18},{3,19},{4,20},{5,21},{6,22},{7,23},{8,24},{9,... | collective-permute-start | bytes 24584 | tf_op jit(solution)/shard_map/ppermute | solution.py:208
  67.0 36.3 %all-to-all-start.1 = ((bf16[32,64,128]{2,1,0:T(8,128)(2,1)}), bf16[32,64,128]{2,1,0:T(8,128)(2,1)S(1)}, u32[]{:S(2)}, u32[]{:S(2)}) async-start(bf16[32,64,128]{2,1,0:T(8,128)(2,1)} %conv.1), calls=%async_computation.1 | async-start | bytes 1048576 | tf_op jit(solution)/shard_map/all_to_all | solution.py:266
  71.3 6.4 %collective-permute-start.1 = (f32[8,1,128]{2,1,0:T(1,128)S(1)}, f32[8,1,128]{2,1,0:T(1,128)S(1)}, u32[]{:S(2)}, u32[]{:S(2)}) collective-permute-start(f32[8,1,128]{2,1,0:T(1,128)S(1)} %broadcast_select_fusion.2), channel_id=1, source_target_pairs={{0,8},{1,9},{2,10},{3,11},{4,12},{5,13},{6,14},{7,15},{8,0},{9,1},... | collective-permute-start | bytes 12296 | tf_op jit(solution)/shard_map/ppermute | solution.py:208
  77.7 5.5 %collective-permute-start.2 = (f32[4,1,128]{2,1,0:T(1,128)S(1)}, f32[4,1,128]{2,1,0:T(1,128)S(1)}, u32[]{:S(2)}, u32[]{:S(2)}) collective-permute-start(f32[4,1,128]{2,1,0:T(1,128)S(1)} %broadcast_select_fusion.4), channel_id=1, source_target_pairs={{0,4},{1,5},{2,6},{3,7},{4,0},{5,1},{6,2},{7,3},{8,12},{9,13},{10,... | collective-permute-start | bytes 6152 | tf_op jit(solution)/shard_map/ppermute | solution.py:208
  83.2 7.0 %collective-permute-start.3 = (f32[2,1,128]{2,1,0:T(1,128)S(1)}, f32[2,1,128]{2,1,0:T(1,128)S(1)}, u32[]{:S(2)}, u32[]{:S(2)}) collective-permute-start(f32[2,1,128]{2,1,0:T(1,128)S(1)} %broadcast_select_fusion.6), channel_id=1, source_target_pairs={{0,2},{1,3},{2,0},{3,1},{4,6},{5,7},{6,4},{7,5},{8,10},{9,11},{10,... | collective-permute-start | bytes 3080 | tf_op jit(solution)/shard_map/ppermute | solution.py:208
  90.2 3.1 %collective-permute-start.4 = (f32[1,1,128]{2,1,0:T(1,128)S(1)}, f32[1,1,128]{2,1,0:T(1,128)S(1)}, u32[]{:S(2)}, u32[]{:S(2)}) collective-permute-start(f32[1,1,128]{2,1,0:T(1,128)S(1)} %broadcast_select_fusion.8), channel_id=1, source_target_pairs={{0,1},{1,0},{2,3},{3,2},{4,5},{5,4},{6,7},{7,6},{8,9},{9,8},{10,11... | collective-permute-start | bytes 1544 | tf_op jit(solution)/shard_map/ppermute | solution.py:208

commit v2 on v1

--- a/solution.py
+++ b/solution.py
@@ -20,11 +20,11 @@
 PARTS = 4
 
 
-def call(kernel, out_shape, flops, moved, outs=VMEM, limit=16, **kw):
+def call(kernel, out_shape, flops, moved, outs, limit=16, **kw):
     return pl.pallas_call(
         kernel,
         out_shape=out_shape,
-        out_specs=jax.tree.map(lambda _: outs, out_shape),
+        out_specs=outs,
         cost_estimate=pl.CostEstimate(flops=flops, bytes_accessed=moved, transcendentals=0),
         compiler_params=pltpu.CompilerParams(vmem_limit_bytes=limit * 2**20),
         **kw,
@@ -69,10 +69,9 @@
         copy.wait()
 
 
-def band_kernel(f_ref, e_ref):
-    length = f_ref.shape[1]
-    filt = f_ref[...].astype(F32)
-    ext = jnp.concatenate([jnp.zeros((1, BLK), F32), filt], axis=1)
+def fill_band(taps, e_ref):
+    length = taps.shape[1]
+    ext = jnp.concatenate([jnp.zeros((1, BLK), F32), taps.astype(F32)], axis=1)
     width = length + BLK
     wide = jnp.broadcast_to(ext, (8, width))
     row = lax.broadcasted_iota(jnp.int32, (8, width), 0)
@@ -105,7 +104,8 @@
     ref[:, half * CPG : (half + 1) * CPG, :] = both.reshape(pieces, CPG, 128)
 
 
-def conv_kernel(in_ref, e_ref, out_ref, held_ref, x_ref, acc_ref, sem):
+def conv_kernel(in_ref, f_ref, out_ref, held_ref, e_ref, x_ref, acc_ref, sem):
+    fill_band(f_ref[...], e_ref)
     nblocks = in_ref.shape[0] // 2
     x_ref[...] = rows_of(in_ref, 0)
     for d in range(nblocks):
@@ -142,7 +142,8 @@
     second.wait()
 
 
-def lag_kernel(scale, in_ref, out_ref, xt_ref, g_ref, s_ref):
+def lag_kernel(scale, in_ref, out_ref, me_ref, xt_ref, g_ref, s_ref):
+    me_ref[...] = jnp.full(me_ref.shape, lax.axis_index("dp"), jnp.int32)
     nblocks = in_ref.shape[0] // 2
     total = nblocks * CPG
     length = nblocks * BLK
@@ -197,12 +198,11 @@
         copy.wait()
 
 
-def halve(terms, replicas):
-    me = lax.axis_index("dp")
+def halve(terms, me, replicas):
     bit = replicas // 2
     while bit:
         both = terms.reshape(2, bit, 1, 128)
-        high = (me & bit) != 0
+        high = jnp.broadcast_to((me & bit) != 0, (bit, 1, 128))
         kept = jnp.where(high, both[1], both[0])
         away = jnp.where(high, both[0], both[1])
         got = lax.ppermute(away, "dp", [(i, i ^ bit) for i in range(replicas)])
@@ -237,14 +237,6 @@
         ],
         name="gate",
     )(*flat)
-    band = call(
-        band_kernel,
-        jax.ShapeDtypeStruct((BLK, length), BF16),
-        BLK * length * 2,
-        BLK * length * 2,
-        in_specs=[VMEM],
-        name="band",
-    )(filters)
     owned = lax.all_to_all(sent, "ctx", split_axis=0, concat_axis=0, tiled=True)
     work = 2 * CPG * length * length
     result = call(
@@ -256,12 +248,13 @@
         in_specs=[VMEM] * 2,
         scratch_shapes=[
             pltpu.VMEM(held.shape, BF16),
+            pltpu.VMEM((BLK, length), BF16),
             pltpu.VMEM((nblocks * CPG, BLK), BF16),
             pltpu.VMEM((nblocks * CPG, BLK), F32),
             DMA((2,)),
         ],
         name="conv",
-    )(owned, band)
+    )(owned, filters)
     owned, result = lax.optimization_barrier((owned, result))
     back = lax.all_to_all(result, "ctx", split_axis=0, concat_axis=0, tiled=True)
     scale = 1.0 / math.sqrt(seqcount * replicas * length * CPG)
@@ -271,9 +264,13 @@
 
     lags_of = call(
         lag_body,
-        jax.ShapeDtypeStruct((length // 128, 1, 128), F32),
+        (
+            jax.ShapeDtypeStruct((length // 128, 1, 128), F32),
+            jax.ShapeDtypeStruct((1, 128), jnp.int32),
+        ),
         work,
         size + BLK * length * 8,
+        (VMEM, VMEM),
         in_specs=[VMEM],
         scratch_shapes=[
             pltpu.VMEM((BLK, nblocks * CPG), BF16),
@@ -282,19 +279,20 @@
         ],
         name="lags",
     )
-    lags = lags_of(owned)
-    grad_filter = halve(lags, replicas)
+    lags, me = lags_of(owned)
+    grad_filter = halve(lags, me, replicas)
     wide = jax.ShapeDtypeStruct((pos, channels), BF16)
-    outs = call(
+    close = call(
         close_kernel,
         (wide,) * 4,
         4 * pos * channels,
         5 * size,
-        ANY,
+        (ANY,) * 4,
         in_specs=[VMEM] * 5,
         scratch_shapes=[pltpu.VMEM((4, pos, channels), BF16), DMA((PARTS, 4))],
         name="close",
-    )(back, *flat)
+    )
+    outs = close(back, *flat)
     return tuple(o.reshape(seqcount, pos, channels) for o in outs) + (grad_filter,)
 
 

time: 105 us -> 105 us (level)
  blocking collectives: 0 us -> 51.7 us
  waiting for transfers between devices: 51.2 us -> 19.6 us
  starting transfers between devices: 43.3 us -> 23.9 us
    all_to_all x0 -> x1, blocking collectives: none -> 51.7 us  [step(): owned = lax.all_to_all(sent, 'ctx', split_axis=0, concat_axis=0, tiled=True)]
    all_to_all x1 -> x0, waiting for transfers between devices: 31.6 us -> none  [step(): owned = lax.all_to_all(sent, 'ctx', split_axis=0, concat_axis=0, tiled=True)]
    all_to_all x1 -> x0, starting transfers between devices: 19.5 us -> none  [step(): owned = lax.all_to_all(sent, 'ctx', split_axis=0, concat_axis=0, tiled=True)]
    pallas_call x3 -> x2, Pallas kernels: 3.96 us -> 3.43 us  [the longest x1 2.26 us: step(): lags, me = lags_of(owned)]
  transfers between devices with their start and end apart: 7 -> 6, of which waited for: 6 -> 5; matrix products, arithmetic and copies ran while one was open for 1% -> 1% of each run, Pallas kernels for 1% -> 0%
where the time goes in v2:
time: 105 us
  blocking collectives  51.7 us (49%)
  starting transfers between devices  23.9 us (23%)
  waiting for transfers between devices  19.6 us (19%)
  Pallas kernels  8.25 us (8%)
    all_to_all x1, blocking collectives, step(): owned = lax.all_to_all(sent, 'ctx', split_axis=0, concat_axis=0, tiled=True)  51.7 us
    ppermute x5, starting transfers between devices, halve(): got = lax.ppermute(away, 'dp', [(i, i ^ bit) for i in range(replicas)])  19.6 us
    ppermute x5, waiting for transfers between devices, halve(): got = lax.ppermute(away, 'dp', [(i, i ^ bit) for i in range(replicas)])  10 us
    all_to_all x1, waiting for transfers between devices, step(): lax.all_to_all(result, 'ctx', split_axis=0, concat_axis=0, tiled=True)  9.56 us
    all_to_all x1, starting transfers between devices, step(): lax.all_to_all(result, 'ctx', split_axis=0, concat_axis=0, tiled=True)  4.36 us
    pallas_call x1, Pallas kernels, step(): call(conv_kernel, held, 2 * work, 2 * size + BLK * length * 2, ANY, in_sp...  2.49 us
    pallas_call x1, Pallas kernels, step(): call(gate_kernel, held, 2 * pos * channels, 3 * size, ANY, 56, in_specs=[...  2.32 us
    pallas_call x1, Pallas kernels, step(): lags, me = lags_of(owned)  2.26 us
  transfers between devices with their start and end apart: 6, of which 5 were waited for; matrix products, arithmetic and copies ran while one was open for 1% of the time, Pallas kernels for 0%

profile of v2, /device:TPU:64, one launch (start us, length us, event | category | flops | bytes accessed | tf_op | source)
XLA Modules:
  0.0 104.9 jit_solution(12258554540437164452)
XLA Ops:
  0.6 2.3 %gate.1 = bf16[32,64,128]{2,1,0:T(8,128)(2,1)} custom-call(bf16[128,1024]{1,0:T(8,128)(2,1)} %bitcast.25, bf16[128,1024]{1,0:T(8,128)(2,1)} %bitcast.27, bf16[128,1024]{1,0:T(8,128)(2,1)} %bitcast.29, bf16[128,1024]{1,0:T(8,128)(2,1)} %bitcast.31), custom_call_target="tpu_custom_call" | custom-call | flops 262144 | bytes 1572864 | tf_op jit(solution)/shard_map/gate/pallas_call | solution.py:224
  3.0 0.0 copy-start.4
  3.0 51.7 %all_to_all.10.in_ref.refs_0_ = bf16[32,64,128]{2,1,0:T(8,128)(2,1)S(1)} all-to-all(bf16[32,64,128]{2,1,0:T(8,128)(2,1)} %gate.1), channel_id=1, replica_groups=mesh['ctx'=32,'dp'=32] {'ctx'}, dimensions={0} | all-to-all | bytes 1048576 | tf_op jit(solution)/shard_map/all_to_all | solution.py:240
  54.7 0.0 copy-done.4
  54.7 2.5 %conv.1 = bf16[32,64,128]{2,1,0:T(8,128)(2,1)} custom-call(bf16[32,64,128]{2,1,0:T(8,128)(2,1)S(1)} %all_to_all.10.in_ref.refs_0_, bf16[1,4096]{1,0:T(2,128)(2,1)S(1)} %copy-done.4), custom_call_target="tpu_custom_call" | custom-call | flops 2147483648 | bytes 3145728 | tf_op jit(solution)/shard_map/conv/pallas_call | solution.py:242
  57.2 2.3 %lags.1 = (f32[32,1,128]{2,1,0:T(1,128)S(1)}, s32[1,128]{1,0:T(1,128)S(1)}) custom-call(bf16[32,64,128]{2,1,0:T(8,128)(2,1)S(1)} %all_to_all.10.in_ref.refs_0_), custom_call_target="tpu_custom_call" | custom-call | flops 1073741824 | bytes 8912896 | tf_op jit(solution)/shard_map/lags/pallas_call | solution.py:282
  59.5 7.7 %collective-permute-start = (f32[16,1,128]{2,1,0:T(1,128)S(1)}, f32[16,1,128]{2,1,0:T(1,128)S(1)}, u32[]{:S(2)}, u32[]{:S(2)}) collective-permute-start(f32[16,1,128]{2,1,0:T(1,128)S(1)} %broadcast_select_fusion), channel_id=1, source_target_pairs={{0,16},{1,17},{2,18},{3,19},{4,20},{5,21},{6,22},{7,23},{8,24},{9,... | collective-permute-start | bytes 24584 | tf_op jit(solution)/shard_map/ppermute | solution.py:208
  67.2 0.0 copy-start
  67.2 0.0 copy-start.1
  67.2 0.0 copy-start.2
  67.2 0.0 copy-start.3
  67.3 4.4 %all-to-all-start.1 = ((bf16[32,64,128]{2,1,0:T(8,128)(2,1)}), bf16[32,64,128]{2,1,0:T(8,128)(2,1)S(1)}, u32[]{:S(2)}, u32[]{:S(2)}) async-start(bf16[32,64,128]{2,1,0:T(8,128)(2,1)} %conv.1), calls=%async_computation.1 | async-start | bytes 1048576 | tf_op jit(solution)/shard_map/all_to_all | solution.py:259
  71.6 0.0 collective-permute-done
  71.7 2.7 %collective-permute-start.1 = (f32[8,1,128]{2,1,0:T(1,128)S(1)}, f32[8,1,128]{2,1,0:T(1,128)S(1)}, u32[]{:S(2)}, u32[]{:S(2)}) collective-permute-start(f32[8,1,128]{2,1,0:T(1,128)S(1)} %broadcast_select_fusion.2), channel_id=1, source_target_pairs={{0,8},{1,9},{2,10},{3,11},{4,12},{5,13},{6,14},{7,15},{8,0},{9,1},... | collective-permute-start | bytes 12296 | tf_op jit(solution)/shard_map/ppermute | solution.py:208
  74.4 3.7 %collective-permute-done.1 = f32[8,1,128]{2,1,0:T(1,128)S(1)} collective-permute-done((f32[8,1,128]{2,1,0:T(1,128)S(1)}, f32[8,1,128]{2,1,0:T(1,128)S(1)}, u32[]{:S(2)}, u32[]{:S(2)}) %collective-permute-start.1) | collective-permute-done | bytes 4128 | tf_op jit(solution)/shard_map/ppermute | solution.py:208
  78.1 2.6 %collective-permute-start.2 = (f32[4,1,128]{2,1,0:T(1,128)S(1)}, f32[4,1,128]{2,1,0:T(1,128)S(1)}, u32[]{:S(2)}, u32[]{:S(2)}) collective-permute-start(f32[4,1,128]{2,1,0:T(1,128)S(1)} %broadcast_select_fusion.4), channel_id=1, source_target_pairs={{0,4},{1,5},{2,6},{3,7},{4,0},{5,1},{6,2},{7,3},{8,12},{9,13},{10,... | collective-permute-start | bytes 6152 | tf_op jit(solution)/shard_map/ppermute | solution.py:208
  80.7 2.9 %collective-permute-done.2 = f32[4,1,128]{2,1,0:T(1,128)S(1)} collective-permute-done((f32[4,1,128]{2,1,0:T(1,128)S(1)}, f32[4,1,128]{2,1,0:T(1,128)S(1)}, u32[]{:S(2)}, u32[]{:S(2)}) %collective-permute-start.2) | collective-permute-done | bytes 2080 | tf_op jit(solution)/shard_map/ppermute | solution.py:208
  83.6 4.6 %collective-permute-start.3 = (f32[2,1,128]{2,1,0:T(1,128)S(1)}, f32[2,1,128]{2,1,0:T(1,128)S(1)}, u32[]{:S(2)}, u32[]{:S(2)}) collective-permute-start(f32[2,1,128]{2,1,0:T(1,128)S(1)} %broadcast_select_fusion.6), channel_id=1, source_target_pairs={{0,2},{1,3},{2,0},{3,1},{4,6},{5,7},{6,4},{7,5},{8,10},{9,11},{10,... | collective-permute-start | bytes 3080 | tf_op jit(solution)/shard_map/ppermute | solution.py:208
  88.2 2.3 %collective-permute-done.3 = f32[2,1,128]{2,1,0:T(1,128)S(1)} collective-permute-done((f32[2,1,128]{2,1,0:T(1,128)S(1)}, f32[2,1,128]{2,1,0:T(1,128)S(1)}, u32[]{:S(2)}, u32[]{:S(2)}) %collective-permute-start.3) | collective-permute-done | bytes 1056 | tf_op jit(solution)/shard_map/ppermute | solution.py:208
  90.6 1.9 %collective-permute-start.4 = (f32[1,1,128]{2,1,0:T(1,128)S(1)}, f32[1,1,128]{2,1,0:T(1,128)S(1)}, u32[]{:S(2)}, u32[]{:S(2)}) collective-permute-start(f32[1,1,128]{2,1,0:T(1,128)S(1)} %bitcast_select_fusion), channel_id=1, source_target_pairs={{0,1},{1,0},{2,3},{3,2},{4,5},{5,4},{6,7},{7,6},{8,9},{9,8},{10,11... | collective-permute-start | bytes 1544 | tf_op jit(solution)/shard_map/ppermute | solution.py:208
  92.5 1.1 %collective-permute-done.4 = f32[1,1,128]{2,1,0:T(1,128)S(1)} collective-permute-done((f32[1,1,128]{2,1,0:T(1,128)S(1)}, f32[1,1,128]{2,1,0:T(1,128)S(1)}, u32[]{:S(2)}, u32[]{:S(2)}) %collective-permute-start.4) | collective-permute-done | bytes 544 | tf_op jit(solution)/shard_map/ppermute | solution.py:208
  93.6 0.5 fusion.5
  94.1 9.6 %all-to-all-done.1.in_ref = bf16[32,64,128]{2,1,0:T(8,128)(2,1)S(1)} async-done(((bf16[32,64,128]{2,1,0:T(8,128)(2,1)}), bf16[32,64,128]{2,1,0:T(8,128)(2,1)S(1)}, u32[]{:S(2)}, u32[]{:S(2)}) %all-to-all-start.1) | async-done | bytes 524320 | tf_op jit(solution)/shard_map/all_to_all | solution.py:259
  103.7 1.2 %close.1 = (bf16[128,1024]{1,0:T(8,128)(2,1)}, bf16[128,1024]{1,0:T(8,128)(2,1)}, bf16[128,1024]{1,0:T(8,128)(2,1)}, bf16[128,1024]{1,0:T(8,128)(2,1)}) custom-call(bf16[32,64,128]{2,1,0:T(8,128)(2,1)S(1)} %all-to-all-done.1.in_ref, bf16[128,1024]{1,0:T(8,128)(2,1)S(1)} %bitcast.26, bf16[128,1024]{1,0:T(8,128)(2,1)S(1)} %bitcast.28, ...), custom_call_target="tpu_custom_call" | custom-call | flops 524288 | bytes 2621440 | tf_op jit(solution)/shard_map/close/pallas_call | solution.py:295
  (14 shorter events, 0.1 us)
Async XLA Ops:
  3.0 51.7 %copy-start.4 = (bf16[1,4096]{1,0:T(2,128)(2,1)S(1)}, bf16[1,4096]{1,0:T(2,128)(2,1)}, u32[]{:S(2)}) copy-start(bf16[1,4096]{1,0:T(2,128)(2,1)} %f_ref.1) | copy-start | bytes 24580
  59.5 12.2 %collective-permute-start = (f32[16,1,128]{2,1,0:T(1,128)S(1)}, f32[16,1,128]{2,1,0:T(1,128)S(1)}, u32[]{:S(2)}, u32[]{:S(2)}) collective-permute-start(f32[16,1,128]{2,1,0:T(1,128)S(1)} %broadcast_select_fusion), channel_id=1, source_target_pairs={{0,16},{1,17},{2,18},{3,19},{4,20},{5,21},{6,22},{7,23},{8,24},{9,... | collective-permute-start | bytes 24584 | tf_op jit(solution)/shard_map/ppermute | solution.py:208
  67.2 36.5 %copy-start = (bf16[1,128,1024]{2,1,0:T(8,128)(2,1)S(1)}, bf16[1,128,1024]{2,1,0:T(8,128)(2,1)}, u32[]{:S(2)}) copy-start(bf16[1,128,1024]{2,1,0:T(8,128)(2,1)} %param.6) | copy-start | bytes 786436
  67.2 36.5 %copy-start.1 = (bf16[1,128,1024]{2,1,0:T(8,128)(2,1)S(1)}, bf16[1,128,1024]{2,1,0:T(8,128)(2,1)}, u32[]{:S(2)}) copy-start(bf16[1,128,1024]{2,1,0:T(8,128)(2,1)} %param.7) | copy-start | bytes 786436
  67.2 36.5 %copy-start.2 = (bf16[1,128,1024]{2,1,0:T(8,128)(2,1)S(1)}, bf16[1,128,1024]{2,1,0:T(8,128)(2,1)}, u32[]{:S(2)}) copy-start(bf16[1,128,1024]{2,1,0:T(8,128)(2,1)} %param.5) | copy-start | bytes 786436
  67.2 36.5 %copy-start.3 = (bf16[1,128,1024]{2,1,0:T(8,128)(2,1)S(1)}, bf16[1,128,1024]{2,1,0:T(8,128)(2,1)}, u32[]{:S(2)}) copy-start(bf16[1,128,1024]{2,1,0:T(8,128)(2,1)} %param.8) | copy-start | bytes 786436
  67.3 36.4 %all-to-all-start.1 = ((bf16[32,64,128]{2,1,0:T(8,128)(2,1)}), bf16[32,64,128]{2,1,0:T(8,128)(2,1)S(1)}, u32[]{:S(2)}, u32[]{:S(2)}) async-start(bf16[32,64,128]{2,1,0:T(8,128)(2,1)} %conv.1), calls=%async_computation.1 | async-start | bytes 1048576 | tf_op jit(solution)/shard_map/all_to_all | solution.py:259
  71.7 6.4 %collective-permute-start.1 = (f32[8,1,128]{2,1,0:T(1,128)S(1)}, f32[8,1,128]{2,1,0:T(1,128)S(1)}, u32[]{:S(2)}, u32[]{:S(2)}) collective-permute-start(f32[8,1,128]{2,1,0:T(1,128)S(1)} %broadcast_select_fusion.2), channel_id=1, source_target_pairs={{0,8},{1,9},{2,10},{3,11},{4,12},{5,13},{6,14},{7,15},{8,0},{9,1},... | collective-permute-start | bytes 12296 | tf_op jit(solution)/shard_map/ppermute | solution.py:208
  78.1 5.5 %collective-permute-start.2 = (f32[4,1,128]{2,1,0:T(1,128)S(1)}, f32[4,1,128]{2,1,0:T(1,128)S(1)}, u32[]{:S(2)}, u32[]{:S(2)}) collective-permute-start(f32[4,1,128]{2,1,0:T(1,128)S(1)} %broadcast_select_fusion.4), channel_id=1, source_target_pairs={{0,4},{1,5},{2,6},{3,7},{4,0},{5,1},{6,2},{7,3},{8,12},{9,13},{10,... | collective-permute-start | bytes 6152 | tf_op jit(solution)/shard_map/ppermute | solution.py:208
  83.6 7.0 %collective-permute-start.3 = (f32[2,1,128]{2,1,0:T(1,128)S(1)}, f32[2,1,128]{2,1,0:T(1,128)S(1)}, u32[]{:S(2)}, u32[]{:S(2)}) collective-permute-start(f32[2,1,128]{2,1,0:T(1,128)S(1)} %broadcast_select_fusion.6), channel_id=1, source_target_pairs={{0,2},{1,3},{2,0},{3,1},{4,6},{5,7},{6,4},{7,5},{8,10},{9,11},{10,... | collective-permute-start | bytes 3080 | tf_op jit(solution)/shard_map/ppermute | solution.py:208
  90.6 3.1 %collective-permute-start.4 = (f32[1,1,128]{2,1,0:T(1,128)S(1)}, f32[1,1,128]{2,1,0:T(1,128)S(1)}, u32[]{:S(2)}, u32[]{:S(2)}) collective-permute-start(f32[1,1,128]{2,1,0:T(1,128)S(1)} %bitcast_select_fusion), channel_id=1, source_target_pairs={{0,1},{1,0},{2,3},{3,2},{4,5},{5,4},{6,7},{7,6},{8,9},{9,8},{10,11... | collective-permute-start | bytes 1544 | tf_op jit(solution)/shard_map/ppermute | solution.py:208

commit v3 on v2

--- a/solution.py
+++ b/solution.py
@@ -31,42 +31,35 @@
     )
 
 
-def gate_kernel(k_ref, v_ref, q_ref, g_ref, out_ref, wide_ref, held_ref, in_sem, out_sem):
+def gate_kernel(
+    k_ref, v_ref, q_ref, g_ref, f_ref, out_ref, e_ref, wide_ref, taps_ref, in_sem, f_sem
+):
     groups, _, pos = out_ref.shape
     step = groups // PARTS
     span = step * CPG
-    pairs = ((k_ref, v_ref), (g_ref, q_ref))
+    taps = pltpu.make_async_copy(f_ref, taps_ref, f_sem)
+    taps.start()
     loads = []
     for part in range(PARTS):
         at = pl.ds(part * span, span)
         row = [
-            [
-                pltpu.make_async_copy(
-                    ref.at[:, at], wide_ref.at[2 * h + j, :, at], in_sem.at[part, 2 * h + j]
-                )
-                for j, ref in enumerate(pair)
-            ]
-            for h, pair in enumerate(pairs)
+            pltpu.make_async_copy(ref.at[:, at], wide_ref.at[i, :, at], in_sem.at[part, i])
+            for i, ref in enumerate((k_ref, v_ref, g_ref, q_ref))
         ]
-        for pair in row:
-            for copy in pair:
-                copy.start()
+        for copy in row:
+            copy.start()
         loads.append(row)
-    stores = []
+    taps.wait()
+    fill_band(taps_ref[...], e_ref)
     for part in range(PARTS):
-        mine = pl.ds(part * step, step)
+        for copy in loads[part]:
+            copy.wait()
+        at = slice(part * span, (part + 1) * span)
+        mine = slice(part * step, (part + 1) * step)
         for h in range(2):
-            for copy in loads[part][h]:
-                copy.wait()
-            at = slice(part * span, (part + 1) * span)
             one = wide_ref[2 * h, :, at].astype(F32) * wide_ref[2 * h + 1, :, at].astype(F32)
             rows = one.astype(BF16).T.reshape(step, CPG, pos)
-            held_ref[part * step : (part + 1) * step, h * CPG : (h + 1) * CPG, :] = rows
-        copy = pltpu.make_async_copy(held_ref.at[mine], out_ref.at[mine], out_sem.at[part])
-        copy.start()
-        stores.append(copy)
-    for copy in stores:
-        copy.wait()
+            out_ref[mine, h * CPG : (h + 1) * CPG, :] = rows
 
 
 def fill_band(taps, e_ref):
@@ -74,10 +67,7 @@
     ext = jnp.concatenate([jnp.zeros((1, BLK), F32), taps.astype(F32)], axis=1)
     width = length + BLK
     wide = jnp.broadcast_to(ext, (8, width))
-    row = lax.broadcasted_iota(jnp.int32, (8, width), 0)
-    base = wide
-    for r in range(1, 8):
-        base = jnp.where(row == r, pltpu.roll(wide, r, 1), base)
+    base = roll_rows(wide, 1)
     prev = None
     for q in range(16):
         cur = base if q == 0 else pltpu.roll(base, 8 * q, 1)
@@ -104,8 +94,7 @@
     ref[:, half * CPG : (half + 1) * CPG, :] = both.reshape(pieces, CPG, 128)
 
 
-def conv_kernel(in_ref, f_ref, out_ref, held_ref, e_ref, x_ref, acc_ref, sem):
-    fill_band(f_ref[...], e_ref)
+def conv_kernel(in_ref, e_ref, out_ref, held_ref, x_ref, acc_ref, sem):
     nblocks = in_ref.shape[0] // 2
     x_ref[...] = rows_of(in_ref, 0)
     for d in range(nblocks):
@@ -142,33 +131,40 @@
     second.wait()
 
 
+def roll_rows(rows, sign):
+    width = rows.shape[1]
+    row = lax.broadcasted_iota(jnp.int32, rows.shape, 0)
+    for bit in (1, 2, 4):
+        rows = jnp.where((row & bit) != 0, pltpu.roll(rows, (sign * bit) % width, 1), rows)
+    return rows
+
+
 def lag_kernel(scale, in_ref, out_ref, me_ref, xt_ref, g_ref, s_ref):
     me_ref[...] = jnp.full(me_ref.shape, lax.axis_index("dp"), jnp.int32)
-    nblocks = in_ref.shape[0] // 2
-    total = nblocks * CPG
-    length = nblocks * BLK
-    xt_ref[...] = rows_of(in_ref, 0).T
-    g_ref[:total, :] = rows_of(in_ref, 1)
-    g_ref[total:, :] = jnp.zeros((128, BLK), BF16)
-    s_ref[:, length:] = jnp.zeros((BLK, 128), F32)
-    for d in range(nblocks):
+    pieces = in_ref.shape[0]
+    total = pieces * CPG
+    length = pieces * 128
+    xt_ref[...] = in_ref[:, :CPG, :].reshape(total, 128).T
+    grads = in_ref[:, CPG:, :].reshape(total, 128)
+    g_ref[:total, :128] = grads
+    g_ref[: total - CPG, 128:] = grads[CPG:]
+    g_ref[total - CPG :, 128:] = jnp.zeros((g_ref.shape[0] - total + CPG, 128), BF16)
+    g_ref[total:, :128] = jnp.zeros((g_ref.shape[0] - total, 128), BF16)
+    s_ref[:, length:] = jnp.zeros((128, 128), F32)
+    for d in range(0, pieces, 2):
         n = -(-(total - d * CPG) // 128) * 128
-        s_ref[:, d * BLK : (d + 1) * BLK] = jnp.dot(
+        s_ref[:, d * 128 : (d + 2) * 128] = jnp.dot(
             xt_ref[:, :n], g_ref[d * CPG : d * CPG + n, :], preferred_element_type=F32
         )
     width = length + 128
-    zeros = jnp.zeros((8, 128), F32)
-    acc = None
-    for q in range(15, -1, -1):
-        low = s_ref[8 * q : 8 * q + 8, :length]
-        high = s_ref[128 + 8 * q : 128 + 8 * q + 8, 128:]
-        term = jnp.concatenate([low + high, zeros], axis=1)
-        acc = term if acc is None else pltpu.roll(acc, width - 8, 1) + term
-    row = lax.broadcasted_iota(jnp.int32, (8, width), 0)
-    lined = acc
-    for r in range(1, 8):
-        lined = jnp.where(row == r, pltpu.roll(acc, width - r, 1), lined)
-    sums = jnp.sum(lined, axis=0, keepdims=True) * scale
+    terms = [s_ref[8 * q : 8 * q + 8, :] for q in range(16)]
+    shift = 8
+    while len(terms) > 1:
+        terms = [
+            terms[i] + pltpu.roll(terms[i + 1], width - shift, 1) for i in range(0, len(terms), 2)
+        ]
+        shift *= 2
+    sums = jnp.sum(roll_rows(terms[0], -1), axis=0, keepdims=True) * scale
     for i in range(length // 128):
         out_ref[i] = sums[:, 128 * i : 128 * (i + 1)]
 
@@ -221,22 +217,21 @@
     flat = [a.reshape(pos, channels) for a in (key_in, value, query, cotangent)]
     held = jax.ShapeDtypeStruct((groups, 2 * CPG, pos), BF16)
     size = groups * 2 * CPG * pos * 2
-    sent = call(
+    sent, band = call(
         gate_kernel,
-        held,
+        (held, jax.ShapeDtypeStruct((BLK, length), BF16)),
         2 * pos * channels,
         3 * size,
-        ANY,
-        56,
-        in_specs=[ANY] * 4,
+        (VMEM, VMEM),
+        in_specs=[ANY] * 5,
         scratch_shapes=[
             pltpu.VMEM((4, pos, channels), BF16),
-            pltpu.VMEM(held.shape, BF16),
+            pltpu.VMEM((1, length), BF16),
             DMA((PARTS, 4)),
-            DMA((PARTS,)),
+            DMA,
         ],
         name="gate",
-    )(*flat)
+    )(*[pltpu.with_memory_space_constraint(a, pltpu.HBM) for a in (*flat, filters)])
     owned = lax.all_to_all(sent, "ctx", split_axis=0, concat_axis=0, tiled=True)
     work = 2 * CPG * length * length
     result = call(
@@ -248,13 +243,12 @@
         in_specs=[VMEM] * 2,
         scratch_shapes=[
             pltpu.VMEM(held.shape, BF16),
-            pltpu.VMEM((BLK, length), BF16),
             pltpu.VMEM((nblocks * CPG, BLK), BF16),
             pltpu.VMEM((nblocks * CPG, BLK), F32),
             DMA((2,)),
         ],
         name="conv",
-    )(owned, filters)
+    )(owned, band)
     owned, result = lax.optimization_barrier((owned, result))
     back = lax.all_to_all(result, "ctx", split_axis=0, concat_axis=0, tiled=True)
     scale = 1.0 / math.sqrt(seqcount * replicas * length * CPG)
@@ -273,9 +267,9 @@
         (VMEM, VMEM),
         in_specs=[VMEM],
         scratch_shapes=[
-            pltpu.VMEM((BLK, nblocks * CPG), BF16),
-            pltpu.VMEM((nblocks * CPG + 128, BLK), BF16),
-            pltpu.VMEM((BLK, length + 128), F32),
+            pltpu.VMEM((128, pieces * CPG), BF16),
+            pltpu.VMEM((pieces * CPG + 128, 256), BF16),
+            pltpu.VMEM((128, length + 128), F32),
         ],
         name="lags",
     )

time: 105 us -> 104 us (level)
  Pallas kernels: 8.25 us -> 7.11 us
where the time goes in v3:
time: 104 us; the launch traced here: 103 us
  blocking collectives  51.5 us (50%)
  starting transfers between devices  23.8 us (23%)
  waiting for transfers between devices  19.6 us (19%)
  Pallas kernels  7.11 us (7%)
    all_to_all x1, blocking collectives, step(): owned = lax.all_to_all(sent, 'ctx', split_axis=0, concat_axis=0, tiled=True)  51.5 us
    ppermute x5, starting transfers between devices, halve(): got = lax.ppermute(away, 'dp', [(i, i ^ bit) for i in range(replicas)])  19.6 us
    ppermute x5, waiting for transfers between devices, halve(): got = lax.ppermute(away, 'dp', [(i, i ^ bit) for i in range(replicas)])  10 us
    all_to_all x1, waiting for transfers between devices, step(): lax.all_to_all(result, 'ctx', split_axis=0, concat_axis=0, tiled=True)  9.56 us
    all_to_all x1, starting transfers between devices, step(): lax.all_to_all(result, 'ctx', split_axis=0, concat_axis=0, tiled=True)  4.22 us
    pallas_call x1, Pallas kernels, step(): call(gate_kernel, (held, jax.ShapeDtypeStruct((BLK, length), BF16)), 2 *...  2.27 us
    pallas_call x1, Pallas kernels, step(): call(conv_kernel, held, 2 * work, 2 * size + BLK * length * 2, ANY, in_sp...  2.23 us
  transfers between devices with their start and end apart: 6, of which 5 were waited for; matrix products, arithmetic and copies ran while one was open for 1% of the time, Pallas kernels for 0%

profile of v3, /device:TPU:64, one launch (start us, length us, event | category | flops | bytes accessed | tf_op | source)
XLA Modules:
  0.0 103.4 jit_solution(17532727892187183873)
XLA Ops:
  0.6 2.3 %gate.1 = (bf16[32,64,128]{2,1,0:T(8,128)(2,1)S(1)}, bf16[256,4096]{1,0:T(8,128)(2,1)S(1)}) custom-call(bf16[128,1024]{1,0:T(8,128)(2,1)} %bitcast.25, bf16[128,1024]{1,0:T(8,128)(2,1)} %bitcast.27, bf16[128,1024]{1,0:T(8,128)(2,1)} %bitcast.29, bf16[128,1024]{1,0:T(8,128)(2,1)} %bitcast.31, bf16[1,4096]{1,0:T(2,128)(2,1)} %f_ref.1), custom_call_target="tpu_custom_call" | custom-call | flops 262144 | bytes 1572864 | tf_op jit(solution)/shard_map/gate/pallas_call | solution.py:220
  2.9 51.5 %all_to_all.10.in_ref.refs_0_ = bf16[32,64,128]{2,1,0:T(8,128)(2,1)S(1)} all-to-all(bf16[32,64,128]{2,1,0:T(8,128)(2,1)S(1)} %get-tuple-element.15), channel_id=1, replica_groups=mesh['ctx'=32,'dp'=32] {'ctx'}, dimensions={0} | all-to-all | bytes 1048576 | tf_op jit(solution)/shard_map/all_to_all | solution.py:235
  54.4 2.2 %conv.1 = bf16[32,64,128]{2,1,0:T(8,128)(2,1)} custom-call(bf16[32,64,128]{2,1,0:T(8,128)(2,1)S(1)} %all_to_all.10.in_ref.refs_0_, bf16[256,4096]{1,0:T(8,128)(2,1)S(1)} %get-tuple-element.16.e_ref), custom_call_target="tpu_custom_call" | custom-call | flops 2147483648 | bytes 3145728 | tf_op jit(solution)/shard_map/conv/pallas_call | solution.py:237
  56.6 0.0 copy-start
  56.6 0.0 copy-start.1
  56.7 0.0 copy-start.2
  56.7 0.0 copy-start.3
  56.7 1.4 %lags.1 = (f32[32,1,128]{2,1,0:T(1,128)S(1)}, s32[1,128]{1,0:T(1,128)S(1)}) custom-call(bf16[32,64,128]{2,1,0:T(8,128)(2,1)S(1)} %all_to_all.10.in_ref.refs_0_), custom_call_target="tpu_custom_call" | custom-call | flops 1073741824 | bytes 8912896 | tf_op jit(solution)/shard_map/lags/pallas_call | solution.py:276
  58.2 7.7 %collective-permute-start = (f32[16,1,128]{2,1,0:T(1,128)S(1)}, f32[16,1,128]{2,1,0:T(1,128)S(1)}, u32[]{:S(2)}, u32[]{:S(2)}) collective-permute-start(f32[16,1,128]{2,1,0:T(1,128)S(1)} %broadcast_select_fusion), channel_id=1, source_target_pairs={{0,16},{1,17},{2,18},{3,19},{4,20},{5,21},{6,22},{7,23},{8,24},{9,... | collective-permute-start | bytes 24584 | tf_op jit(solution)/shard_map/ppermute | solution.py:204
  65.9 4.2 %all-to-all-start.1 = ((bf16[32,64,128]{2,1,0:T(8,128)(2,1)}), bf16[32,64,128]{2,1,0:T(8,128)(2,1)S(1)}, u32[]{:S(2)}, u32[]{:S(2)}) async-start(bf16[32,64,128]{2,1,0:T(8,128)(2,1)} %conv.1), calls=%async_computation.1 | async-start | bytes 1048576 | tf_op jit(solution)/shard_map/all_to_all | solution.py:253
  70.1 0.0 collective-permute-done
  70.2 2.7 %collective-permute-start.1 = (f32[8,1,128]{2,1,0:T(1,128)S(1)}, f32[8,1,128]{2,1,0:T(1,128)S(1)}, u32[]{:S(2)}, u32[]{:S(2)}) collective-permute-start(f32[8,1,128]{2,1,0:T(1,128)S(1)} %broadcast_select_fusion.2), channel_id=1, source_target_pairs={{0,8},{1,9},{2,10},{3,11},{4,12},{5,13},{6,14},{7,15},{8,0},{9,1},... | collective-permute-start | bytes 12296 | tf_op jit(solution)/shard_map/ppermute | solution.py:204
  72.9 3.7 %collective-permute-done.1 = f32[8,1,128]{2,1,0:T(1,128)S(1)} collective-permute-done((f32[8,1,128]{2,1,0:T(1,128)S(1)}, f32[8,1,128]{2,1,0:T(1,128)S(1)}, u32[]{:S(2)}, u32[]{:S(2)}) %collective-permute-start.1) | collective-permute-done | bytes 4128 | tf_op jit(solution)/shard_map/ppermute | solution.py:204
  76.6 2.6 %collective-permute-start.2 = (f32[4,1,128]{2,1,0:T(1,128)S(1)}, f32[4,1,128]{2,1,0:T(1,128)S(1)}, u32[]{:S(2)}, u32[]{:S(2)}) collective-permute-start(f32[4,1,128]{2,1,0:T(1,128)S(1)} %broadcast_select_fusion.4), channel_id=1, source_target_pairs={{0,4},{1,5},{2,6},{3,7},{4,0},{5,1},{6,2},{7,3},{8,12},{9,13},{10,... | collective-permute-start | bytes 6152 | tf_op jit(solution)/shard_map/ppermute | solution.py:204
  79.2 2.9 %collective-permute-done.2 = f32[4,1,128]{2,1,0:T(1,128)S(1)} collective-permute-done((f32[4,1,128]{2,1,0:T(1,128)S(1)}, f32[4,1,128]{2,1,0:T(1,128)S(1)}, u32[]{:S(2)}, u32[]{:S(2)}) %collective-permute-start.2) | collective-permute-done | bytes 2080 | tf_op jit(solution)/shard_map/ppermute | solution.py:204
  82.1 4.6 %collective-permute-start.3 = (f32[2,1,128]{2,1,0:T(1,128)S(1)}, f32[2,1,128]{2,1,0:T(1,128)S(1)}, u32[]{:S(2)}, u32[]{:S(2)}) collective-permute-start(f32[2,1,128]{2,1,0:T(1,128)S(1)} %broadcast_select_fusion.6), channel_id=1, source_target_pairs={{0,2},{1,3},{2,0},{3,1},{4,6},{5,7},{6,4},{7,5},{8,10},{9,11},{10,... | collective-permute-start | bytes 3080 | tf_op jit(solution)/shard_map/ppermute | solution.py:204
  86.7 2.3 %collective-permute-done.3 = f32[2,1,128]{2,1,0:T(1,128)S(1)} collective-permute-done((f32[2,1,128]{2,1,0:T(1,128)S(1)}, f32[2,1,128]{2,1,0:T(1,128)S(1)}, u32[]{:S(2)}, u32[]{:S(2)}) %collective-permute-start.3) | collective-permute-done | bytes 1056 | tf_op jit(solution)/shard_map/ppermute | solution.py:204
  89.1 1.9 %collective-permute-start.4 = (f32[1,1,128]{2,1,0:T(1,128)S(1)}, f32[1,1,128]{2,1,0:T(1,128)S(1)}, u32[]{:S(2)}, u32[]{:S(2)}) collective-permute-start(f32[1,1,128]{2,1,0:T(1,128)S(1)} %bitcast_select_fusion), channel_id=1, source_target_pairs={{0,1},{1,0},{2,3},{3,2},{4,5},{5,4},{6,7},{7,6},{8,9},{9,8},{10,11... | collective-permute-start | bytes 1544 | tf_op jit(solution)/shard_map/ppermute | solution.py:204
  91.0 1.1 %collective-permute-done.4 = f32[1,1,128]{2,1,0:T(1,128)S(1)} collective-permute-done((f32[1,1,128]{2,1,0:T(1,128)S(1)}, f32[1,1,128]{2,1,0:T(1,128)S(1)}, u32[]{:S(2)}, u32[]{:S(2)}) %collective-permute-start.4) | collective-permute-done | bytes 544 | tf_op jit(solution)/shard_map/ppermute | solution.py:204
  92.1 0.5 fusion.5
  92.7 9.6 %all-to-all-done.1.in_ref = bf16[32,64,128]{2,1,0:T(8,128)(2,1)S(1)} async-done(((bf16[32,64,128]{2,1,0:T(8,128)(2,1)}), bf16[32,64,128]{2,1,0:T(8,128)(2,1)S(1)}, u32[]{:S(2)}, u32[]{:S(2)}) %all-to-all-start.1) | async-done | bytes 524320 | tf_op jit(solution)/shard_map/all_to_all | solution.py:253
  102.2 0.0 copy-done
  102.2 0.0 copy-done.1
  102.2 1.2 %close.1 = (bf16[128,1024]{1,0:T(8,128)(2,1)}, bf16[128,1024]{1,0:T(8,128)(2,1)}, bf16[128,1024]{1,0:T(8,128)(2,1)}, bf16[128,1024]{1,0:T(8,128)(2,1)}) custom-call(bf16[32,64,128]{2,1,0:T(8,128)(2,1)S(1)} %all-to-all-done.1.in_ref, bf16[128,1024]{1,0:T(8,128)(2,1)S(1)} %bitcast.26, bf16[128,1024]{1,0:T(8,128)(2,1)S(1)} %bitcast.28, ...), custom_call_target="tpu_custom_call" | custom-call | flops 524288 | bytes 2621440 | tf_op jit(solution)/shard_map/close/pallas_call | solution.py:289
  (12 shorter events, 0.1 us)
Async XLA Ops:
  56.6 45.6 %copy-start = (bf16[1,128,1024]{2,1,0:T(8,128)(2,1)S(1)}, bf16[1,128,1024]{2,1,0:T(8,128)(2,1)}, u32[]{:S(2)}) copy-start(bf16[1,128,1024]{2,1,0:T(8,128)(2,1)} %param.6) | copy-start | bytes 786436
  56.6 45.6 %copy-start.1 = (bf16[1,128,1024]{2,1,0:T(8,128)(2,1)S(1)}, bf16[1,128,1024]{2,1,0:T(8,128)(2,1)}, u32[]{:S(2)}) copy-start(bf16[1,128,1024]{2,1,0:T(8,128)(2,1)} %param.7) | copy-start | bytes 786436
  56.7 45.6 %copy-start.2 = (bf16[1,128,1024]{2,1,0:T(8,128)(2,1)S(1)}, bf16[1,128,1024]{2,1,0:T(8,128)(2,1)}, u32[]{:S(2)}) copy-start(bf16[1,128,1024]{2,1,0:T(8,128)(2,1)} %param.5) | copy-start | bytes 786436
  56.7 45.6 %copy-start.3 = (bf16[1,128,1024]{2,1,0:T(8,128)(2,1)S(1)}, bf16[1,128,1024]{2,1,0:T(8,128)(2,1)}, u32[]{:S(2)}) copy-start(bf16[1,128,1024]{2,1,0:T(8,128)(2,1)} %param.8) | copy-start | bytes 786436
  58.2 12.0 %collective-permute-start = (f32[16,1,128]{2,1,0:T(1,128)S(1)}, f32[16,1,128]{2,1,0:T(1,128)S(1)}, u32[]{:S(2)}, u32[]{:S(2)}) collective-permute-start(f32[16,1,128]{2,1,0:T(1,128)S(1)} %broadcast_select_fusion), channel_id=1, source_target_pairs={{0,16},{1,17},{2,18},{3,19},{4,20},{5,21},{6,22},{7,23},{8,24},{9,... | collective-permute-start | bytes 24584 | tf_op jit(solution)/shard_map/ppermute | solution.py:204
  65.9 36.3 %all-to-all-start.1 = ((bf16[32,64,128]{2,1,0:T(8,128)(2,1)}), bf16[32,64,128]{2,1,0:T(8,128)(2,1)S(1)}, u32[]{:S(2)}, u32[]{:S(2)}) async-start(bf16[32,64,128]{2,1,0:T(8,128)(2,1)} %conv.1), calls=%async_computation.1 | async-start | bytes 1048576 | tf_op jit(solution)/shard_map/all_to_all | solution.py:253
  70.2 6.4 %collective-permute-start.1 = (f32[8,1,128]{2,1,0:T(1,128)S(1)}, f32[8,1,128]{2,1,0:T(1,128)S(1)}, u32[]{:S(2)}, u32[]{:S(2)}) collective-permute-start(f32[8,1,128]{2,1,0:T(1,128)S(1)} %broadcast_select_fusion.2), channel_id=1, source_target_pairs={{0,8},{1,9},{2,10},{3,11},{4,12},{5,13},{6,14},{7,15},{8,0},{9,1},... | collective-permute-start | bytes 12296 | tf_op jit(solution)/shard_map/ppermute | solution.py:204
  76.6 5.5 %collective-permute-start.2 = (f32[4,1,128]{2,1,0:T(1,128)S(1)}, f32[4,1,128]{2,1,0:T(1,128)S(1)}, u32[]{:S(2)}, u32[]{:S(2)}) collective-permute-start(f32[4,1,128]{2,1,0:T(1,128)S(1)} %broadcast_select_fusion.4), channel_id=1, source_target_pairs={{0,4},{1,5},{2,6},{3,7},{4,0},{5,1},{6,2},{7,3},{8,12},{9,13},{10,... | collective-permute-start | bytes 6152 | tf_op jit(solution)/shard_map/ppermute | solution.py:204
  82.1 7.0 %collective-permute-start.3 = (f32[2,1,128]{2,1,0:T(1,128)S(1)}, f32[2,1,128]{2,1,0:T(1,128)S(1)}, u32[]{:S(2)}, u32[]{:S(2)}) collective-permute-start(f32[2,1,128]{2,1,0:T(1,128)S(1)} %broadcast_select_fusion.6), channel_id=1, source_target_pairs={{0,2},{1,3},{2,0},{3,1},{4,6},{5,7},{6,4},{7,5},{8,10},{9,11},{10,... | collective-permute-start | bytes 3080 | tf_op jit(solution)/shard_map/ppermute | solution.py:204
  89.1 3.1 %collective-permute-start.4 = (f32[1,1,128]{2,1,0:T(1,128)S(1)}, f32[1,1,128]{2,1,0:T(1,128)S(1)}, u32[]{:S(2)}, u32[]{:S(2)}) collective-permute-start(f32[1,1,128]{2,1,0:T(1,128)S(1)} %bitcast_select_fusion), channel_id=1, source_target_pairs={{0,1},{1,0},{2,3},{3,2},{4,5},{5,4},{6,7},{7,6},{8,9},{9,8},{10,11... | collective-permute-start | bytes 1544 | tf_op jit(solution)/shard_map/ppermute | solution.py:204

commit v4 on v3

--- a/solution.py
+++ b/solution.py
@@ -31,14 +31,10 @@
     )
 
 
-def gate_kernel(
-    k_ref, v_ref, q_ref, g_ref, f_ref, out_ref, e_ref, wide_ref, taps_ref, in_sem, f_sem
-):
+def gate_kernel(k_ref, v_ref, q_ref, g_ref, out_ref, wide_ref, in_sem):
     groups, _, pos = out_ref.shape
     step = groups // PARTS
     span = step * CPG
-    taps = pltpu.make_async_copy(f_ref, taps_ref, f_sem)
-    taps.start()
     loads = []
     for part in range(PARTS):
         at = pl.ds(part * span, span)
@@ -49,8 +45,6 @@
         for copy in row:
             copy.start()
         loads.append(row)
-    taps.wait()
-    fill_band(taps_ref[...], e_ref)
     for part in range(PARTS):
         for copy in loads[part]:
             copy.wait()
@@ -76,8 +70,7 @@
             continue
         pair = jnp.concatenate([prev, cur], axis=0).astype(BF16)
         at = 8 * (q - 1)
-        e_ref[at : at + 16, :] = pair[:, BLK:]
-        e_ref[128 + at : 128 + at + 16, :] = pair[:, 128 : 128 + length]
+        e_ref[at : at + 16, :] = pair[:, 128:]
 
 
 def rows_of(ref, half):
@@ -87,35 +80,49 @@
     return jnp.concatenate([pair[:, 0], pair[:, 1]], axis=-1).reshape(pieces // 2 * CPG, BLK)
 
 
-def put_rows(ref, half, rows):
-    pieces = ref.shape[0]
-    blocks = rows.reshape(pieces // 2, CPG, BLK)
+def put_rows(ref, half, first, rows):
+    count = rows.shape[0] // CPG
+    blocks = rows.reshape(count, CPG, BLK)
     both = jnp.stack([blocks[:, :, :128], blocks[:, :, 128:]], axis=1)
-    ref[:, half * CPG : (half + 1) * CPG, :] = both.reshape(pieces, CPG, 128)
-
-
-def conv_kernel(in_ref, e_ref, out_ref, held_ref, x_ref, acc_ref, sem):
+    into = slice(2 * first, 2 * (first + count))
+    ref[into, half * CPG : (half + 1) * CPG, :] = both.reshape(2 * count, CPG, 128)
+
+
+def conv_kernel(in_ref, f_ref, out_ref, held_ref, e_ref, x_ref, acc_ref, sem):
+    fill_band(f_ref[...], e_ref)
     nblocks = in_ref.shape[0] // 2
+    copies = []
+
+    def finish(half, first, count):
+        rows = acc_ref[first * CPG : (first + count) * CPG, :].astype(BF16)
+        put_rows(held_ref, half, first, rows)
+        at = (pl.ds(2 * first, 2 * count), pl.ds(half * CPG, CPG), slice(None))
+        copy = pltpu.make_async_copy(held_ref.at[at], out_ref.at[at], sem.at[len(copies)])
+        copy.start()
+        copies.append(copy)
+
+    def block(d):
+        at = d * BLK
+        return jnp.concatenate(
+            [e_ref[:, at + 128 : at + 128 + BLK], e_ref[:, at : at + BLK]], axis=0
+        )
+
+    quarter = nblocks // 4
     x_ref[...] = rows_of(in_ref, 0)
     for d in range(nblocks):
         n = (nblocks - d) * CPG
-        part = jnp.dot(
-            x_ref[:n, :], e_ref[:, d * BLK : (d + 1) * BLK], preferred_element_type=F32
-        )
+        part = jnp.dot(x_ref[:n, :], block(d), preferred_element_type=F32)
         if d == 0:
             acc_ref[...] = part
         else:
             acc_ref[d * CPG :, :] += part
-    put_rows(held_ref, 0, acc_ref[...].astype(BF16))
-    half = pl.ds(0, CPG)
-    first = pltpu.make_async_copy(held_ref.at[:, half, :], out_ref.at[:, half, :], sem.at[0])
-    first.start()
+    finish(0, 0, nblocks)
     x_ref[...] = rows_of(in_ref, 1)
     for d in range(nblocks):
         n = (nblocks - d) * CPG
         part = lax.dot_general(
             x_ref[d * CPG :, :],
-            e_ref[:, d * BLK : (d + 1) * BLK],
+            block(d),
             (((1,), (1,)), ((), ())),
             preferred_element_type=F32,
         )
@@ -123,12 +130,11 @@
             acc_ref[...] = part
         else:
             acc_ref[:n, :] += part
-    put_rows(held_ref, 1, acc_ref[...].astype(BF16))
-    half = pl.ds(CPG, CPG)
-    second = pltpu.make_async_copy(held_ref.at[:, half, :], out_ref.at[:, half, :], sem.at[1])
-    second.start()
-    first.wait()
-    second.wait()
+        if (d + 1) % quarter == 0 and d + 1 >= 2 * quarter:
+            count = 2 * quarter if d + 1 == 2 * quarter else quarter
+            finish(1, nblocks - d - 1, count)
+    for copy in copies:
+        copy.wait()
 
 
 def roll_rows(rows, sign):
@@ -198,10 +204,11 @@
     bit = replicas // 2
     while bit:
         both = terms.reshape(2, bit, 1, 128)
+        mask = bit + bit // 2 if bit == replicas // 2 else bit
         high = jnp.broadcast_to((me & bit) != 0, (bit, 1, 128))
         kept = jnp.where(high, both[1], both[0])
         away = jnp.where(high, both[0], both[1])
-        got = lax.ppermute(away, "dp", [(i, i ^ bit) for i in range(replicas)])
+        got = lax.ppermute(away, "dp", [(i, i ^ mask) for i in range(replicas)])
         terms = kept + got
         bit //= 2
     return terms.reshape(1, 128)
@@ -217,21 +224,16 @@
     flat = [a.reshape(pos, channels) for a in (key_in, value, query, cotangent)]
     held = jax.ShapeDtypeStruct((groups, 2 * CPG, pos), BF16)
     size = groups * 2 * CPG * pos * 2
-    sent, band = call(
+    sent = call(
         gate_kernel,
-        (held, jax.ShapeDtypeStruct((BLK, length), BF16)),
+        held,
         2 * pos * channels,
         3 * size,
-        (VMEM, VMEM),
-        in_specs=[ANY] * 5,
-        scratch_shapes=[
-            pltpu.VMEM((4, pos, channels), BF16),
-            pltpu.VMEM((1, length), BF16),
-            DMA((PARTS, 4)),
-            DMA,
-        ],
+        VMEM,
+        in_specs=[ANY] * 4,
+        scratch_shapes=[pltpu.VMEM((4, pos, channels), BF16), DMA((PARTS, 4))],
         name="gate",
-    )(*[pltpu.with_memory_space_constraint(a, pltpu.HBM) for a in (*flat, filters)])
+    )(*[pltpu.with_memory_space_constraint(a, pltpu.HBM) for a in flat])
     owned = lax.all_to_all(sent, "ctx", split_axis=0, concat_axis=0, tiled=True)
     work = 2 * CPG * length * length
     result = call(
@@ -243,12 +245,13 @@
         in_specs=[VMEM] * 2,
         scratch_shapes=[
             pltpu.VMEM(held.shape, BF16),
+            pltpu.VMEM((128, length + 128), BF16),
             pltpu.VMEM((nblocks * CPG, BLK), BF16),
             pltpu.VMEM((nblocks * CPG, BLK), F32),
-            DMA((2,)),
+            DMA((4,)),
         ],
         name="conv",
-    )(owned, band)
+    )(owned, filters)
     owned, result = lax.optimization_barrier((owned, result))
     back = lax.all_to_all(result, "ctx", split_axis=0, concat_axis=0, tiled=True)
     scale = 1.0 / math.sqrt(seqcount * replicas * length * CPG)

time: 104 us -> 103 us (level)
  waiting for transfers between devices: 19.6 us -> 18.3 us
    ppermute x5, waiting for transfers between devices: 10 us -> 8.7 us  [halve(): got = lax.ppermute(away, 'dp', [(i, i ^ mask) for i in range(replicas)])]
    pallas_call x1, Pallas kernels: 2.23 us -> 3.33 us  [step(): call(conv_kernel, held, 2 * work, 2 * size + BLK * length * 2, ANY, in_sp...]
where the time goes in v4:
time: 103 us; the launch traced here: 102 us
  blocking collectives  51.5 us (50%)
  starting transfers between devices  23.7 us (23%)
  waiting for transfers between devices  18.3 us (18%)
  Pallas kernels  7.44 us (7%)
    all_to_all x1, blocking collectives, step(): owned = lax.all_to_all(sent, 'ctx', split_axis=0, concat_axis=0, tiled=True)  51.5 us
    ppermute x5, starting transfers between devices, halve(): got = lax.ppermute(away, 'dp', [(i, i ^ mask) for i in range(replicas)])  19.3 us
    all_to_all x1, waiting for transfers between devices, step(): lax.all_to_all(result, 'ctx', split_axis=0, concat_axis=0, tiled=True)  9.56 us
    ppermute x5, waiting for transfers between devices, halve(): got = lax.ppermute(away, 'dp', [(i, i ^ mask) for i in range(replicas)])  8.7 us
    all_to_all x1, starting transfers between devices, step(): lax.all_to_all(result, 'ctx', split_axis=0, concat_axis=0, tiled=True)  4.37 us
    pallas_call x1, Pallas kernels, step(): call(conv_kernel, held, 2 * work, 2 * size + BLK * length * 2, ANY, in_sp...  3.33 us
  transfers between devices with their start and end apart: 6, of which 5 were waited for; matrix products, arithmetic and copies ran while one was open for 1% of the time, Pallas kernels for 0%

profile of v4, /device:TPU:64, one launch (start us, length us, event | category | flops | bytes accessed | tf_op | source)
XLA Modules:
  0.0 102.3 jit_solution(16389521759415251524)
XLA Ops:
  0.6 1.5 %gate.1 = bf16[32,64,128]{2,1,0:T(8,128)(2,1)S(1)} custom-call(bf16[128,1024]{1,0:T(8,128)(2,1)} %bitcast.25, bf16[128,1024]{1,0:T(8,128)(2,1)} %bitcast.27, bf16[128,1024]{1,0:T(8,128)(2,1)} %bitcast.29, bf16[128,1024]{1,0:T(8,128)(2,1)} %bitcast.31), custom_call_target="tpu_custom_call" | custom-call | flops 262144 | bytes 1572864 | tf_op jit(solution)/shard_map/gate/pallas_call | solution.py:227
  2.1 0.0 copy-start.4
  2.2 51.5 %all_to_all.10.in_ref.refs_0_ = bf16[32,64,128]{2,1,0:T(8,128)(2,1)S(1)} all-to-all(bf16[32,64,128]{2,1,0:T(8,128)(2,1)S(1)} %gate.1), channel_id=1, replica_groups=mesh['ctx'=32,'dp'=32] {'ctx'}, dimensions={0} | all-to-all | bytes 1048576 | tf_op jit(solution)/shard_map/all_to_all | solution.py:237
  53.6 0.0 copy-done.4
  53.6 3.3 %conv.1 = bf16[32,64,128]{2,1,0:T(8,128)(2,1)} custom-call(bf16[32,64,128]{2,1,0:T(8,128)(2,1)S(1)} %all_to_all.10.in_ref.refs_0_, bf16[1,4096]{1,0:T(2,128)(2,1)S(1)} %copy-done.4), custom_call_target="tpu_custom_call" | custom-call | flops 2147483648 | bytes 3145728 | tf_op jit(solution)/shard_map/conv/pallas_call | solution.py:239
  57.0 1.4 %lags.1 = (f32[32,1,128]{2,1,0:T(1,128)S(1)}, s32[1,128]{1,0:T(1,128)S(1)}) custom-call(bf16[32,64,128]{2,1,0:T(8,128)(2,1)S(1)} %all_to_all.10.in_ref.refs_0_), custom_call_target="tpu_custom_call" | custom-call | flops 1073741824 | bytes 8912896 | tf_op jit(solution)/shard_map/lags/pallas_call | solution.py:279
  58.5 6.1 %collective-permute-start = (f32[16,1,128]{2,1,0:T(1,128)S(1)}, f32[16,1,128]{2,1,0:T(1,128)S(1)}, u32[]{:S(2)}, u32[]{:S(2)}) collective-permute-start(f32[16,1,128]{2,1,0:T(1,128)S(1)} %broadcast_select_fusion), channel_id=1, source_target_pairs={{0,24},{1,25},{2,26},{3,27},{4,28},{5,29},{6,30},{7,31},{8,16},{9,... | collective-permute-start | bytes 24584 | tf_op jit(solution)/shard_map/ppermute | solution.py:211
  64.6 0.0 copy-start
  64.6 0.0 copy-start.1
  64.6 0.0 copy-start.2
  64.7 0.0 copy-start.3
  64.7 4.4 %all-to-all-start.1 = ((bf16[32,64,128]{2,1,0:T(8,128)(2,1)}), bf16[32,64,128]{2,1,0:T(8,128)(2,1)S(1)}, u32[]{:S(2)}, u32[]{:S(2)}) async-start(bf16[32,64,128]{2,1,0:T(8,128)(2,1)} %conv.1), calls=%async_computation.1 | async-start | bytes 1048576 | tf_op jit(solution)/shard_map/all_to_all | solution.py:256
  69.0 0.0 collective-permute-done
  69.1 4.0 %collective-permute-start.1 = (f32[8,1,128]{2,1,0:T(1,128)S(1)}, f32[8,1,128]{2,1,0:T(1,128)S(1)}, u32[]{:S(2)}, u32[]{:S(2)}) collective-permute-start(f32[8,1,128]{2,1,0:T(1,128)S(1)} %broadcast_select_fusion.2), channel_id=1, source_target_pairs={{0,8},{1,9},{2,10},{3,11},{4,12},{5,13},{6,14},{7,15},{8,0},{9,1},... | collective-permute-start | bytes 12296 | tf_op jit(solution)/shard_map/ppermute | solution.py:211
  73.1 2.4 %collective-permute-done.1 = f32[8,1,128]{2,1,0:T(1,128)S(1)} collective-permute-done((f32[8,1,128]{2,1,0:T(1,128)S(1)}, f32[8,1,128]{2,1,0:T(1,128)S(1)}, u32[]{:S(2)}, u32[]{:S(2)}) %collective-permute-start.1) | collective-permute-done | bytes 4128 | tf_op jit(solution)/shard_map/ppermute | solution.py:211
  75.5 2.6 %collective-permute-start.2 = (f32[4,1,128]{2,1,0:T(1,128)S(1)}, f32[4,1,128]{2,1,0:T(1,128)S(1)}, u32[]{:S(2)}, u32[]{:S(2)}) collective-permute-start(f32[4,1,128]{2,1,0:T(1,128)S(1)} %broadcast_select_fusion.4), channel_id=1, source_target_pairs={{0,4},{1,5},{2,6},{3,7},{4,0},{5,1},{6,2},{7,3},{8,12},{9,13},{10,... | collective-permute-start | bytes 6152 | tf_op jit(solution)/shard_map/ppermute | solution.py:211
  78.1 2.9 %collective-permute-done.2 = f32[4,1,128]{2,1,0:T(1,128)S(1)} collective-permute-done((f32[4,1,128]{2,1,0:T(1,128)S(1)}, f32[4,1,128]{2,1,0:T(1,128)S(1)}, u32[]{:S(2)}, u32[]{:S(2)}) %collective-permute-start.2) | collective-permute-done | bytes 2080 | tf_op jit(solution)/shard_map/ppermute | solution.py:211
  81.0 4.6 %collective-permute-start.3 = (f32[2,1,128]{2,1,0:T(1,128)S(1)}, f32[2,1,128]{2,1,0:T(1,128)S(1)}, u32[]{:S(2)}, u32[]{:S(2)}) collective-permute-start(f32[2,1,128]{2,1,0:T(1,128)S(1)} %broadcast_select_fusion.6), channel_id=1, source_target_pairs={{0,2},{1,3},{2,0},{3,1},{4,6},{5,7},{6,4},{7,5},{8,10},{9,11},{10,... | collective-permute-start | bytes 3080 | tf_op jit(solution)/shard_map/ppermute | solution.py:211
  85.6 2.3 %collective-permute-done.3 = f32[2,1,128]{2,1,0:T(1,128)S(1)} collective-permute-done((f32[2,1,128]{2,1,0:T(1,128)S(1)}, f32[2,1,128]{2,1,0:T(1,128)S(1)}, u32[]{:S(2)}, u32[]{:S(2)}) %collective-permute-start.3) | collective-permute-done | bytes 1056 | tf_op jit(solution)/shard_map/ppermute | solution.py:211
  88.0 1.9 %collective-permute-start.4 = (f32[1,1,128]{2,1,0:T(1,128)S(1)}, f32[1,1,128]{2,1,0:T(1,128)S(1)}, u32[]{:S(2)}, u32[]{:S(2)}) collective-permute-start(f32[1,1,128]{2,1,0:T(1,128)S(1)} %bitcast_select_fusion), channel_id=1, source_target_pairs={{0,1},{1,0},{2,3},{3,2},{4,5},{5,4},{6,7},{7,6},{8,9},{9,8},{10,11... | collective-permute-start | bytes 1544 | tf_op jit(solution)/shard_map/ppermute | solution.py:211
  89.9 1.1 %collective-permute-done.4 = f32[1,1,128]{2,1,0:T(1,128)S(1)} collective-permute-done((f32[1,1,128]{2,1,0:T(1,128)S(1)}, f32[1,1,128]{2,1,0:T(1,128)S(1)}, u32[]{:S(2)}, u32[]{:S(2)}) %collective-permute-start.4) | collective-permute-done | bytes 544 | tf_op jit(solution)/shard_map/ppermute | solution.py:211
  91.0 0.5 fusion.5
  91.6 9.6 %all-to-all-done.1.in_ref = bf16[32,64,128]{2,1,0:T(8,128)(2,1)S(1)} async-done(((bf16[32,64,128]{2,1,0:T(8,128)(2,1)}), bf16[32,64,128]{2,1,0:T(8,128)(2,1)S(1)}, u32[]{:S(2)}, u32[]{:S(2)}) %all-to-all-start.1) | async-done | bytes 524320 | tf_op jit(solution)/shard_map/all_to_all | solution.py:256
  101.1 1.2 %close.1 = (bf16[128,1024]{1,0:T(8,128)(2,1)}, bf16[128,1024]{1,0:T(8,128)(2,1)}, bf16[128,1024]{1,0:T(8,128)(2,1)}, bf16[128,1024]{1,0:T(8,128)(2,1)}) custom-call(bf16[32,64,128]{2,1,0:T(8,128)(2,1)S(1)} %all-to-all-done.1.in_ref, bf16[128,1024]{1,0:T(8,128)(2,1)S(1)} %bitcast.26, bf16[128,1024]{1,0:T(8,128)(2,1)S(1)} %bitcast.28, ...), custom_call_target="tpu_custom_call" | custom-call | flops 524288 | bytes 2621440 | tf_op jit(solution)/shard_map/close/pallas_call | solution.py:292
  (14 shorter events, 0.1 us)
Async XLA Ops:
  2.1 51.5 %copy-start.4 = (bf16[1,4096]{1,0:T(2,128)(2,1)S(1)}, bf16[1,4096]{1,0:T(2,128)(2,1)}, u32[]{:S(2)}) copy-start(bf16[1,4096]{1,0:T(2,128)(2,1)} %f_ref.1) | copy-start | bytes 24580
  58.5 10.6 %collective-permute-start = (f32[16,1,128]{2,1,0:T(1,128)S(1)}, f32[16,1,128]{2,1,0:T(1,128)S(1)}, u32[]{:S(2)}, u32[]{:S(2)}) collective-permute-start(f32[16,1,128]{2,1,0:T(1,128)S(1)} %broadcast_select_fusion), channel_id=1, source_target_pairs={{0,24},{1,25},{2,26},{3,27},{4,28},{5,29},{6,30},{7,31},{8,16},{9,... | collective-permute-start | bytes 24584 | tf_op jit(solution)/shard_map/ppermute | solution.py:211
  64.6 36.5 %copy-start = (bf16[1,128,1024]{2,1,0:T(8,128)(2,1)S(1)}, bf16[1,128,1024]{2,1,0:T(8,128)(2,1)}, u32[]{:S(2)}) copy-start(bf16[1,128,1024]{2,1,0:T(8,128)(2,1)} %param.6) | copy-start | bytes 786436
  64.6 36.5 %copy-start.1 = (bf16[1,128,1024]{2,1,0:T(8,128)(2,1)S(1)}, bf16[1,128,1024]{2,1,0:T(8,128)(2,1)}, u32[]{:S(2)}) copy-start(bf16[1,128,1024]{2,1,0:T(8,128)(2,1)} %param.7) | copy-start | bytes 786436
  64.6 36.5 %copy-start.2 = (bf16[1,128,1024]{2,1,0:T(8,128)(2,1)S(1)}, bf16[1,128,1024]{2,1,0:T(8,128)(2,1)}, u32[]{:S(2)}) copy-start(bf16[1,128,1024]{2,1,0:T(8,128)(2,1)} %param.5) | copy-start | bytes 786436
  64.7 36.5 %copy-start.3 = (bf16[1,128,1024]{2,1,0:T(8,128)(2,1)S(1)}, bf16[1,128,1024]{2,1,0:T(8,128)(2,1)}, u32[]{:S(2)}) copy-start(bf16[1,128,1024]{2,1,0:T(8,128)(2,1)} %param.8) | copy-start | bytes 786436
  64.7 36.5 %all-to-all-start.1 = ((bf16[32,64,128]{2,1,0:T(8,128)(2,1)}), bf16[32,64,128]{2,1,0:T(8,128)(2,1)S(1)}, u32[]{:S(2)}, u32[]{:S(2)}) async-start(bf16[32,64,128]{2,1,0:T(8,128)(2,1)} %conv.1), calls=%async_computation.1 | async-start | bytes 1048576 | tf_op jit(solution)/shard_map/all_to_all | solution.py:256
  69.1 6.4 %collective-permute-start.1 = (f32[8,1,128]{2,1,0:T(1,128)S(1)}, f32[8,1,128]{2,1,0:T(1,128)S(1)}, u32[]{:S(2)}, u32[]{:S(2)}) collective-permute-start(f32[8,1,128]{2,1,0:T(1,128)S(1)} %broadcast_select_fusion.2), channel_id=1, source_target_pairs={{0,8},{1,9},{2,10},{3,11},{4,12},{5,13},{6,14},{7,15},{8,0},{9,1},... | collective-permute-start | bytes 12296 | tf_op jit(solution)/shard_map/ppermute | solution.py:211
  75.5 5.5 %collective-permute-start.2 = (f32[4,1,128]{2,1,0:T(1,128)S(1)}, f32[4,1,128]{2,1,0:T(1,128)S(1)}, u32[]{:S(2)}, u32[]{:S(2)}) collective-permute-start(f32[4,1,128]{2,1,0:T(1,128)S(1)} %broadcast_select_fusion.4), channel_id=1, source_target_pairs={{0,4},{1,5},{2,6},{3,7},{4,0},{5,1},{6,2},{7,3},{8,12},{9,13},{10,... | collective-permute-start | bytes 6152 | tf_op jit(solution)/shard_map/ppermute | solution.py:211
  81.0 7.0 %collective-permute-start.3 = (f32[2,1,128]{2,1,0:T(1,128)S(1)}, f32[2,1,128]{2,1,0:T(1,128)S(1)}, u32[]{:S(2)}, u32[]{:S(2)}) collective-permute-start(f32[2,1,128]{2,1,0:T(1,128)S(1)} %broadcast_select_fusion.6), channel_id=1, source_target_pairs={{0,2},{1,3},{2,0},{3,1},{4,6},{5,7},{6,4},{7,5},{8,10},{9,11},{10,... | collective-permute-start | bytes 3080 | tf_op jit(solution)/shard_map/ppermute | solution.py:211
  88.0 3.1 %collective-permute-start.4 = (f32[1,1,128]{2,1,0:T(1,128)S(1)}, f32[1,1,128]{2,1,0:T(1,128)S(1)}, u32[]{:S(2)}, u32[]{:S(2)}) collective-permute-start(f32[1,1,128]{2,1,0:T(1,128)S(1)} %bitcast_select_fusion), channel_id=1, source_target_pairs={{0,1},{1,0},{2,3},{3,2},{4,5},{5,4},{6,7},{7,6},{8,9},{9,8},{10,11... | collective-permute-start | bytes 1544 | tf_op jit(solution)/shard_map/ppermute | solution.py:211

commit v5 on v3

--- a/solution.py
+++ b/solution.py
@@ -31,14 +31,10 @@
     )
 
 
-def gate_kernel(
-    k_ref, v_ref, q_ref, g_ref, f_ref, out_ref, e_ref, wide_ref, taps_ref, in_sem, f_sem
-):
+def gate_kernel(k_ref, v_ref, q_ref, g_ref, out_ref, wide_ref, in_sem):
     groups, _, pos = out_ref.shape
     step = groups // PARTS
     span = step * CPG
-    taps = pltpu.make_async_copy(f_ref, taps_ref, f_sem)
-    taps.start()
     loads = []
     for part in range(PARTS):
         at = pl.ds(part * span, span)
@@ -49,8 +45,6 @@
         for copy in row:
             copy.start()
         loads.append(row)
-    taps.wait()
-    fill_band(taps_ref[...], e_ref)
     for part in range(PARTS):
         for copy in loads[part]:
             copy.wait()
@@ -94,7 +88,8 @@
     ref[:, half * CPG : (half + 1) * CPG, :] = both.reshape(pieces, CPG, 128)
 
 
-def conv_kernel(in_ref, e_ref, out_ref, held_ref, x_ref, acc_ref, sem):
+def conv_kernel(in_ref, f_ref, out_ref, held_ref, e_ref, x_ref, acc_ref, sem):
+    fill_band(f_ref[...], e_ref)
     nblocks = in_ref.shape[0] // 2
     x_ref[...] = rows_of(in_ref, 0)
     for d in range(nblocks):
@@ -170,13 +165,32 @@
 
 
 def close_kernel(
-    in_ref, k_ref, v_ref, q_ref, g_ref, out_ref, gq_ref, gk_ref, gv_ref, held_ref, sem
+    in_ref,
+    k_ref,
+    v_ref,
+    q_ref,
+    g_ref,
+    kept_ref,
+    got_ref,
+    out_ref,
+    gq_ref,
+    gk_ref,
+    gv_ref,
+    gf_ref,
+    held_ref,
+    sum_ref,
+    sem,
+    sum_sem,
 ):
+    sum_ref[...] = kept_ref[0] + got_ref[0]
+    sums = pltpu.make_async_copy(sum_ref, gf_ref, sum_sem)
     groups, _, pos = in_ref.shape
     step = groups // PARTS
     span = step * CPG
     copies = []
     for part in range(PARTS):
+        if part == 1:
+            sums.start()
         at = slice(part * span, (part + 1) * span)
         for h, gates, outs in ((0, (q_ref, g_ref), (out_ref, gq_ref)), (1, (v_ref, k_ref), (gk_ref, gv_ref))):
             rows = in_ref[part * step : (part + 1) * step, h * CPG : (h + 1) * CPG, :]
@@ -192,19 +206,21 @@
                 copies.append(copy)
     for copy in copies:
         copy.wait()
+    sums.wait()
 
 
 def halve(terms, me, replicas):
     bit = replicas // 2
     while bit:
         both = terms.reshape(2, bit, 1, 128)
+        mask = bit + bit // 2 if bit == replicas // 2 else bit
         high = jnp.broadcast_to((me & bit) != 0, (bit, 1, 128))
         kept = jnp.where(high, both[1], both[0])
         away = jnp.where(high, both[0], both[1])
-        got = lax.ppermute(away, "dp", [(i, i ^ bit) for i in range(replicas)])
+        got = lax.ppermute(away, "dp", [(i, i ^ mask) for i in range(replicas)])
         terms = kept + got
         bit //= 2
-    return terms.reshape(1, 128)
+    return kept, got
 
 
 def step(query, key_in, value, cotangent, filters):
@@ -217,21 +233,16 @@
     flat = [a.reshape(pos, channels) for a in (key_in, value, query, cotangent)]
     held = jax.ShapeDtypeStruct((groups, 2 * CPG, pos), BF16)
     size = groups * 2 * CPG * pos * 2
-    sent, band = call(
+    sent = call(
         gate_kernel,
-        (held, jax.ShapeDtypeStruct((BLK, length), BF16)),
+        held,
         2 * pos * channels,
         3 * size,
-        (VMEM, VMEM),
-        in_specs=[ANY] * 5,
-        scratch_shapes=[
-            pltpu.VMEM((4, pos, channels), BF16),
-            pltpu.VMEM((1, length), BF16),
-            DMA((PARTS, 4)),
-            DMA,
-        ],
+        VMEM,
+        in_specs=[ANY] * 4,
+        scratch_shapes=[pltpu.VMEM((4, pos, channels), BF16), DMA((PARTS, 4))],
         name="gate",
-    )(*[pltpu.with_memory_space_constraint(a, pltpu.HBM) for a in (*flat, filters)])
+    )(*[pltpu.with_memory_space_constraint(a, pltpu.HBM) for a in flat])
     owned = lax.all_to_all(sent, "ctx", split_axis=0, concat_axis=0, tiled=True)
     work = 2 * CPG * length * length
     result = call(
@@ -243,12 +254,13 @@
         in_specs=[VMEM] * 2,
         scratch_shapes=[
             pltpu.VMEM(held.shape, BF16),
+            pltpu.VMEM((BLK, length), BF16),
             pltpu.VMEM((nblocks * CPG, BLK), BF16),
             pltpu.VMEM((nblocks * CPG, BLK), F32),
             DMA((2,)),
         ],
         name="conv",
-    )(owned, band)
+    )(owned, filters)
     owned, result = lax.optimization_barrier((owned, result))
     back = lax.all_to_all(result, "ctx", split_axis=0, concat_axis=0, tiled=True)
     scale = 1.0 / math.sqrt(seqcount * replicas * length * CPG)
@@ -274,19 +286,24 @@
         name="lags",
     )
     lags, me = lags_of(owned)
-    grad_filter = halve(lags, me, replicas)
+    last = halve(lags, me, replicas)
     wide = jax.ShapeDtypeStruct((pos, channels), BF16)
     close = call(
         close_kernel,
-        (wide,) * 4,
+        (wide,) * 4 + (jax.ShapeDtypeStruct((1, 128), F32),),
         4 * pos * channels,
         5 * size,
-        (ANY,) * 4,
-        in_specs=[VMEM] * 5,
-        scratch_shapes=[pltpu.VMEM((4, pos, channels), BF16), DMA((PARTS, 4))],
+        (ANY,) * 5,
+        in_specs=[VMEM] * 7,
+        scratch_shapes=[
+            pltpu.VMEM((4, pos, channels), BF16),
+            pltpu.VMEM((1, 128), F32),
+            DMA((PARTS, 4)),
+            DMA,
+        ],
         name="close",
     )
-    outs = close(back, *flat)
+    *outs, grad_filter = close(back, *flat, *last)
     return tuple(o.reshape(seqcount, pos, channels) for o in outs) + (grad_filter,)
 
 

time: 104 us -> 96.8 us (0.931)
  waiting for transfers between devices: 19.6 us -> 11.9 us
    all_to_all x1, waiting for transfers between devices: 9.56 us -> 2.47 us  [step(): lax.all_to_all(result, 'ctx', split_axis=0, concat_axis=0, tiled=True)]
  transfers between devices with their start and end apart: 6 -> 6, of which waited for: 5 -> 6; matrix products, arithmetic and copies ran while one was open for 1% -> 0% of each run, Pallas kernels for 0% -> 0%
where the time goes in v5:
time: 96.8 us; the launch traced here: 96.3 us
  blocking collectives  51.5 us (53%)
  starting transfers between devices  24.7 us (26%)
  waiting for transfers between devices  11.9 us (12%)
  Pallas kernels  7.35 us (8%)
    all_to_all x1, blocking collectives, step(): owned = lax.all_to_all(sent, 'ctx', split_axis=0, concat_axis=0, tiled=True)  51.5 us
    ppermute x5, starting transfers between devices, halve(): got = lax.ppermute(away, 'dp', [(i, i ^ mask) for i in range(replicas)])  20.3 us
    ppermute x5, waiting for transfers between devices, halve(): got = lax.ppermute(away, 'dp', [(i, i ^ mask) for i in range(replicas)])  9.4 us
    all_to_all x1, starting transfers between devices, step(): lax.all_to_all(result, 'ctx', split_axis=0, concat_axis=0, tiled=True)  4.35 us
    pallas_call x1, Pallas kernels, step(): call(conv_kernel, held, 2 * work, 2 * size + BLK * length * 2, ANY, in_sp...  3.23 us
    all_to_all x1, waiting for transfers between devices, step(): lax.all_to_all(result, 'ctx', split_axis=0, concat_axis=0, tiled=True)  2.47 us
  transfers between devices with their start and end apart: 6, of which 6 were waited for; matrix products, arithmetic and copies ran while one was open for 0% of the time, Pallas kernels for 0%

profile of v5, /device:TPU:64, one launch (start us, length us, event | category | flops | bytes accessed | tf_op | source)
XLA Modules:
  0.0 96.3 jit_solution(8071206488884232768)
XLA Ops:
  0.6 1.5 %gate.1 = bf16[32,64,128]{2,1,0:T(8,128)(2,1)S(1)} custom-call(bf16[128,1024]{1,0:T(8,128)(2,1)} %bitcast.19, bf16[128,1024]{1,0:T(8,128)(2,1)} %bitcast.21, bf16[128,1024]{1,0:T(8,128)(2,1)} %bitcast.23, bf16[128,1024]{1,0:T(8,128)(2,1)} %bitcast.25), custom_call_target="tpu_custom_call" | custom-call | flops 262144 | bytes 1572864 | tf_op jit(solution)/shard_map/gate/pallas_call | solution.py:236
  2.1 0.0 copy-start.4
  2.2 51.5 %all_to_all.10.in_ref.refs_0_ = bf16[32,64,128]{2,1,0:T(8,128)(2,1)S(1)} all-to-all(bf16[32,64,128]{2,1,0:T(8,128)(2,1)S(1)} %gate.1), channel_id=1, replica_groups=mesh['ctx'=32,'dp'=32] {'ctx'}, dimensions={0} | all-to-all | bytes 1048576 | tf_op jit(solution)/shard_map/all_to_all | solution.py:246
  53.6 0.0 copy-done.4
  53.6 3.2 %conv.1 = bf16[32,64,128]{2,1,0:T(8,128)(2,1)} custom-call(bf16[32,64,128]{2,1,0:T(8,128)(2,1)S(1)} %all_to_all.10.in_ref.refs_0_, bf16[1,4096]{1,0:T(2,128)(2,1)S(1)} %copy-done.4), custom_call_target="tpu_custom_call" | custom-call | flops 2147483648 | bytes 3145728 | tf_op jit(solution)/shard_map/conv/pallas_call | solution.py:248
  56.9 1.4 %lags.1 = (f32[32,1,128]{2,1,0:T(1,128)S(1)}, s32[1,128]{1,0:T(1,128)S(1)}) custom-call(bf16[32,64,128]{2,1,0:T(8,128)(2,1)S(1)} %all_to_all.10.in_ref.refs_0_), custom_call_target="tpu_custom_call" | custom-call | flops 1073741824 | bytes 8912896 | tf_op jit(solution)/shard_map/lags/pallas_call | solution.py:288
  58.3 0.0 copy-start
  58.4 0.0 copy-start.1
  58.4 0.0 copy-start.2
  58.4 0.0 copy-start.3
  58.4 4.4 %all-to-all-start.1 = ((bf16[32,64,128]{2,1,0:T(8,128)(2,1)}), bf16[32,64,128]{2,1,0:T(8,128)(2,1)S(1)}, u32[]{:S(2)}, u32[]{:S(2)}) async-start(bf16[32,64,128]{2,1,0:T(8,128)(2,1)} %conv.1), calls=%async_computation.1 | async-start | bytes 1048576 | tf_op jit(solution)/shard_map/all_to_all | solution.py:265
  62.8 6.2 %collective-permute-start = (f32[16,1,128]{2,1,0:T(1,128)S(1)}, f32[16,1,128]{2,1,0:T(1,128)S(1)}, u32[]{:S(2)}, u32[]{:S(2)}) collective-permute-start(f32[16,1,128]{2,1,0:T(1,128)S(1)} %broadcast_select_fusion), channel_id=1, source_target_pairs={{0,24},{1,25},{2,26},{3,27},{4,28},{5,29},{6,30},{7,31},{8,16},{9,... | collective-permute-start | bytes 24584 | tf_op jit(solution)/shard_map/ppermute | solution.py:220
  68.9 1.7 %collective-permute-done = f32[16,1,128]{2,1,0:T(1,128)S(1)} collective-permute-done((f32[16,1,128]{2,1,0:T(1,128)S(1)}, f32[16,1,128]{2,1,0:T(1,128)S(1)}, u32[]{:S(2)}, u32[]{:S(2)}) %collective-permute-start) | collective-permute-done | bytes 8224 | tf_op jit(solution)/shard_map/ppermute | solution.py:220
  70.6 4.3 %collective-permute-start.1 = (f32[8,1,128]{2,1,0:T(1,128)S(1)}, f32[8,1,128]{2,1,0:T(1,128)S(1)}, u32[]{:S(2)}, u32[]{:S(2)}) collective-permute-start(f32[8,1,128]{2,1,0:T(1,128)S(1)} %broadcast_select_fusion.2), channel_id=1, source_target_pairs={{0,8},{1,9},{2,10},{3,11},{4,12},{5,13},{6,14},{7,15},{8,0},{9,1},... | collective-permute-start | bytes 12296 | tf_op jit(solution)/shard_map/ppermute | solution.py:220
  75.0 2.1 %collective-permute-done.1 = f32[8,1,128]{2,1,0:T(1,128)S(1)} collective-permute-done((f32[8,1,128]{2,1,0:T(1,128)S(1)}, f32[8,1,128]{2,1,0:T(1,128)S(1)}, u32[]{:S(2)}, u32[]{:S(2)}) %collective-permute-start.1) | collective-permute-done | bytes 4128 | tf_op jit(solution)/shard_map/ppermute | solution.py:220
  77.1 3.3 %collective-permute-start.2 = (f32[4,1,128]{2,1,0:T(1,128)S(1)}, f32[4,1,128]{2,1,0:T(1,128)S(1)}, u32[]{:S(2)}, u32[]{:S(2)}) collective-permute-start(f32[4,1,128]{2,1,0:T(1,128)S(1)} %broadcast_select_fusion.4), channel_id=1, source_target_pairs={{0,4},{1,5},{2,6},{3,7},{4,0},{5,1},{6,2},{7,3},{8,12},{9,13},{10,... | collective-permute-start | bytes 6152 | tf_op jit(solution)/shard_map/ppermute | solution.py:220
  80.4 2.2 %collective-permute-done.2 = f32[4,1,128]{2,1,0:T(1,128)S(1)} collective-permute-done((f32[4,1,128]{2,1,0:T(1,128)S(1)}, f32[4,1,128]{2,1,0:T(1,128)S(1)}, u32[]{:S(2)}, u32[]{:S(2)}) %collective-permute-start.2) | collective-permute-done | bytes 2080 | tf_op jit(solution)/shard_map/ppermute | solution.py:220
  82.6 4.6 %collective-permute-start.3 = (f32[2,1,128]{2,1,0:T(1,128)S(1)}, f32[2,1,128]{2,1,0:T(1,128)S(1)}, u32[]{:S(2)}, u32[]{:S(2)}) collective-permute-start(f32[2,1,128]{2,1,0:T(1,128)S(1)} %broadcast_select_fusion.6), channel_id=1, source_target_pairs={{0,2},{1,3},{2,0},{3,1},{4,6},{5,7},{6,4},{7,5},{8,10},{9,11},{10,... | collective-permute-start | bytes 3080 | tf_op jit(solution)/shard_map/ppermute | solution.py:220
  87.2 2.3 %collective-permute-done.3 = f32[2,1,128]{2,1,0:T(1,128)S(1)} collective-permute-done((f32[2,1,128]{2,1,0:T(1,128)S(1)}, f32[2,1,128]{2,1,0:T(1,128)S(1)}, u32[]{:S(2)}, u32[]{:S(2)}) %collective-permute-start.3) | collective-permute-done | bytes 1056 | tf_op jit(solution)/shard_map/ppermute | solution.py:220
  89.6 1.9 %collective-permute-start.4 = (f32[1,1,128]{2,1,0:T(1,128)S(1)}, f32[1,1,128]{2,1,0:T(1,128)S(1)}, u32[]{:S(2)}, u32[]{:S(2)}) collective-permute-start(f32[1,1,128]{2,1,0:T(1,128)S(1)} %get-tuple-element.23), channel_id=1, source_target_pairs={{0,1},{1,0},{2,3},{3,2},{4,5},{5,4},{6,7},{7,6},{8,9},{9,8},{10,11... | collective-permute-start | bytes 1544 | tf_op jit(solution)/shard_map/ppermute | solution.py:220
  91.5 1.1 %collective-permute-done.4.got_ref = f32[1,1,128]{2,1,0:T(1,128)S(1)} collective-permute-done((f32[1,1,128]{2,1,0:T(1,128)S(1)}, f32[1,1,128]{2,1,0:T(1,128)S(1)}, u32[]{:S(2)}, u32[]{:S(2)}) %collective-permute-start.4) | collective-permute-done | bytes 544 | tf_op jit(solution)/shard_map/ppermute | solution.py:220
  92.6 2.5 %all-to-all-done.1.in_ref = bf16[32,64,128]{2,1,0:T(8,128)(2,1)S(1)} async-done(((bf16[32,64,128]{2,1,0:T(8,128)(2,1)}), bf16[32,64,128]{2,1,0:T(8,128)(2,1)S(1)}, u32[]{:S(2)}, u32[]{:S(2)}) %all-to-all-start.1) | async-done | bytes 524320 | tf_op jit(solution)/shard_map/all_to_all | solution.py:265
  95.1 0.0 copy-done
  95.1 1.2 %close.1 = (bf16[128,1024]{1,0:T(8,128)(2,1)}, bf16[128,1024]{1,0:T(8,128)(2,1)}, bf16[128,1024]{1,0:T(8,128)(2,1)}, bf16[128,1024]{1,0:T(8,128)(2,1)}, f32[1,128]{1,0:T(1,128)}) custom-call(bf16[32,64,128]{2,1,0:T(8,128)(2,1)S(1)} %all-to-all-done.1.in_ref, bf16[128,1024]{1,0:T(8,128)(2,1)S(1)} %bitcast.20, bf16[128,1024]{1,0:T(8,128)(2,1)S(1)} %bitcast.22, ...), custom_call_target="tpu_custom_call" | custom-call | flops 524288 | bytes 2621440 | tf_op jit(solution)/shard_map/close/pallas_call | solution.py:306
  (13 shorter events, 0.1 us)
Async XLA Ops:
  2.1 51.5 %copy-start.4 = (bf16[1,4096]{1,0:T(2,128)(2,1)S(1)}, bf16[1,4096]{1,0:T(2,128)(2,1)}, u32[]{:S(2)}) copy-start(bf16[1,4096]{1,0:T(2,128)(2,1)} %f_ref.1) | copy-start | bytes 24580
  58.3 36.7 %copy-start = (bf16[1,128,1024]{2,1,0:T(8,128)(2,1)S(1)}, bf16[1,128,1024]{2,1,0:T(8,128)(2,1)}, u32[]{:S(2)}) copy-start(bf16[1,128,1024]{2,1,0:T(8,128)(2,1)} %param.6) | copy-start | bytes 786436
  58.4 36.7 %copy-start.1 = (bf16[1,128,1024]{2,1,0:T(8,128)(2,1)S(1)}, bf16[1,128,1024]{2,1,0:T(8,128)(2,1)}, u32[]{:S(2)}) copy-start(bf16[1,128,1024]{2,1,0:T(8,128)(2,1)} %param.7) | copy-start | bytes 786436
  58.4 36.7 %copy-start.2 = (bf16[1,128,1024]{2,1,0:T(8,128)(2,1)S(1)}, bf16[1,128,1024]{2,1,0:T(8,128)(2,1)}, u32[]{:S(2)}) copy-start(bf16[1,128,1024]{2,1,0:T(8,128)(2,1)} %param.5) | copy-start | bytes 786436
  58.4 36.7 %copy-start.3 = (bf16[1,128,1024]{2,1,0:T(8,128)(2,1)S(1)}, bf16[1,128,1024]{2,1,0:T(8,128)(2,1)}, u32[]{:S(2)}) copy-start(bf16[1,128,1024]{2,1,0:T(8,128)(2,1)} %param.8) | copy-start | bytes 786436
  58.4 36.7 %all-to-all-start.1 = ((bf16[32,64,128]{2,1,0:T(8,128)(2,1)}), bf16[32,64,128]{2,1,0:T(8,128)(2,1)S(1)}, u32[]{:S(2)}, u32[]{:S(2)}) async-start(bf16[32,64,128]{2,1,0:T(8,128)(2,1)} %conv.1), calls=%async_computation.1 | async-start | bytes 1048576 | tf_op jit(solution)/shard_map/all_to_all | solution.py:265
  62.8 7.8 %collective-permute-start = (f32[16,1,128]{2,1,0:T(1,128)S(1)}, f32[16,1,128]{2,1,0:T(1,128)S(1)}, u32[]{:S(2)}, u32[]{:S(2)}) collective-permute-start(f32[16,1,128]{2,1,0:T(1,128)S(1)} %broadcast_select_fusion), channel_id=1, source_target_pairs={{0,24},{1,25},{2,26},{3,27},{4,28},{5,29},{6,30},{7,31},{8,16},{9,... | collective-permute-start | bytes 24584 | tf_op jit(solution)/shard_map/ppermute | solution.py:220
  70.6 6.4 %collective-permute-start.1 = (f32[8,1,128]{2,1,0:T(1,128)S(1)}, f32[8,1,128]{2,1,0:T(1,128)S(1)}, u32[]{:S(2)}, u32[]{:S(2)}) collective-permute-start(f32[8,1,128]{2,1,0:T(1,128)S(1)} %broadcast_select_fusion.2), channel_id=1, source_target_pairs={{0,8},{1,9},{2,10},{3,11},{4,12},{5,13},{6,14},{7,15},{8,0},{9,1},... | collective-permute-start | bytes 12296 | tf_op jit(solution)/shard_map/ppermute | solution.py:220
  77.1 5.5 %collective-permute-start.2 = (f32[4,1,128]{2,1,0:T(1,128)S(1)}, f32[4,1,128]{2,1,0:T(1,128)S(1)}, u32[]{:S(2)}, u32[]{:S(2)}) collective-permute-start(f32[4,1,128]{2,1,0:T(1,128)S(1)} %broadcast_select_fusion.4), channel_id=1, source_target_pairs={{0,4},{1,5},{2,6},{3,7},{4,0},{5,1},{6,2},{7,3},{8,12},{9,13},{10,... | collective-permute-start | bytes 6152 | tf_op jit(solution)/shard_map/ppermute | solution.py:220
  82.6 7.0 %collective-permute-start.3 = (f32[2,1,128]{2,1,0:T(1,128)S(1)}, f32[2,1,128]{2,1,0:T(1,128)S(1)}, u32[]{:S(2)}, u32[]{:S(2)}) collective-permute-start(f32[2,1,128]{2,1,0:T(1,128)S(1)} %broadcast_select_fusion.6), channel_id=1, source_target_pairs={{0,2},{1,3},{2,0},{3,1},{4,6},{5,7},{6,4},{7,5},{8,10},{9,11},{10,... | collective-permute-start | bytes 3080 | tf_op jit(solution)/shard_map/ppermute | solution.py:220
  89.6 3.1 %collective-permute-start.4 = (f32[1,1,128]{2,1,0:T(1,128)S(1)}, f32[1,1,128]{2,1,0:T(1,128)S(1)}, u32[]{:S(2)}, u32[]{:S(2)}) collective-permute-start(f32[1,1,128]{2,1,0:T(1,128)S(1)} %get-tuple-element.23), channel_id=1, source_target_pairs={{0,1},{1,0},{2,3},{3,2},{4,5},{5,4},{6,7},{7,6},{8,9},{9,8},{10,11... | collective-permute-start | bytes 1544 | tf_op jit(solution)/shard_map/ppermute | solution.py:220

commit v6 on v5

--- a/solution.py
+++ b/solution.py
@@ -61,7 +61,10 @@
     ext = jnp.concatenate([jnp.zeros((1, BLK), F32), taps.astype(F32)], axis=1)
     width = length + BLK
     wide = jnp.broadcast_to(ext, (8, width))
-    base = roll_rows(wide, 1)
+    row = lax.broadcasted_iota(jnp.int32, (8, width), 0)
+    base = wide
+    for r in range(1, 8):
+        base = jnp.where(row == r, pltpu.roll(wide, r, 1), base)
     prev = None
     for q in range(16):
         cur = base if q == 0 else pltpu.roll(base, 8 * q, 1)
@@ -126,11 +129,11 @@
     second.wait()
 
 
-def roll_rows(rows, sign):
+def roll_rows(rows):
     width = rows.shape[1]
     row = lax.broadcasted_iota(jnp.int32, rows.shape, 0)
     for bit in (1, 2, 4):
-        rows = jnp.where((row & bit) != 0, pltpu.roll(rows, (sign * bit) % width, 1), rows)
+        rows = jnp.where((row & bit) != 0, pltpu.roll(rows, width - bit, 1), rows)
     return rows
 
 
@@ -159,7 +162,7 @@
             terms[i] + pltpu.roll(terms[i + 1], width - shift, 1) for i in range(0, len(terms), 2)
         ]
         shift *= 2
-    sums = jnp.sum(roll_rows(terms[0], -1), axis=0, keepdims=True) * scale
+    sums = jnp.sum(roll_rows(terms[0]), axis=0, keepdims=True) * scale
     for i in range(length // 128):
         out_ref[i] = sums[:, 128 * i : 128 * (i + 1)]
 

time: 96.8 us -> 96 us (level)
  the two profiles are of different devices: /device:TPU:64 before, /device:TPU:96 now
where the time goes in v6:
time: 96 us; the launch traced here: 95.5 us
  blocking collectives  51.5 us (54%)
  starting transfers between devices  18.4 us (19%)
  waiting for transfers between devices  18.1 us (19%)
  Pallas kernels  6.6 us (7%)
    all_to_all x1, blocking collectives, step(): owned = lax.all_to_all(sent, 'ctx', split_axis=0, concat_axis=0, tiled=True)  51.5 us
    ppermute x5, waiting for transfers between devices, halve(): got = lax.ppermute(away, 'dp', [(i, i ^ mask) for i in range(replicas)])  15.5 us
    ppermute x5, starting transfers between devices, halve(): got = lax.ppermute(away, 'dp', [(i, i ^ mask) for i in range(replicas)])  14.1 us
    all_to_all x1, starting transfers between devices, step(): lax.all_to_all(result, 'ctx', split_axis=0, concat_axis=0, tiled=True)  4.35 us
    all_to_all x1, waiting for transfers between devices, step(): lax.all_to_all(result, 'ctx', split_axis=0, concat_axis=0, tiled=True)  2.66 us
    pallas_call x1, Pallas kernels, step(): call(conv_kernel, held, 2 * work, 2 * size + BLK * length * 2, ANY, in_sp...  2.48 us
  transfers between devices with their start and end apart: 6, of which 6 were waited for; matrix products, arithmetic and copies ran while one was open for 0% of the time, Pallas kernels for 0%

profile of v6, /device:TPU:96, one launch (start us, length us, event | category | flops | bytes accessed | tf_op | source)
XLA Modules:
  0.0 95.5 jit_solution(13063897696567771575)
XLA Ops:
  0.6 1.5 %gate.1 = bf16[32,64,128]{2,1,0:T(8,128)(2,1)S(1)} custom-call(bf16[128,1024]{1,0:T(8,128)(2,1)} %bitcast.19, bf16[128,1024]{1,0:T(8,128)(2,1)} %bitcast.21, bf16[128,1024]{1,0:T(8,128)(2,1)} %bitcast.23, bf16[128,1024]{1,0:T(8,128)(2,1)} %bitcast.25), custom_call_target="tpu_custom_call" | custom-call | flops 262144 | bytes 1572864 | tf_op jit(solution)/shard_map/gate/pallas_call | solution.py:239
  2.1 0.0 copy-start.4
  2.2 51.5 %all_to_all.10.in_ref.refs_0_ = bf16[32,64,128]{2,1,0:T(8,128)(2,1)S(1)} all-to-all(bf16[32,64,128]{2,1,0:T(8,128)(2,1)S(1)} %gate.1), channel_id=1, replica_groups=mesh['ctx'=32,'dp'=32] {'ctx'}, dimensions={0} | all-to-all | bytes 1048576 | tf_op jit(solution)/shard_map/all_to_all | solution.py:249
  53.6 0.0 copy-done.4
  53.6 2.5 %conv.1 = bf16[32,64,128]{2,1,0:T(8,128)(2,1)} custom-call(bf16[32,64,128]{2,1,0:T(8,128)(2,1)S(1)} %all_to_all.10.in_ref.refs_0_, bf16[1,4096]{1,0:T(2,128)(2,1)S(1)} %copy-done.4), custom_call_target="tpu_custom_call" | custom-call | flops 2147483648 | bytes 3145728 | tf_op jit(solution)/shard_map/conv/pallas_call | solution.py:251
  56.1 1.4 %lags.1 = (f32[32,1,128]{2,1,0:T(1,128)S(1)}, s32[1,128]{1,0:T(1,128)S(1)}) custom-call(bf16[32,64,128]{2,1,0:T(8,128)(2,1)S(1)} %all_to_all.10.in_ref.refs_0_), custom_call_target="tpu_custom_call" | custom-call | flops 1073741824 | bytes 8912896 | tf_op jit(solution)/shard_map/lags/pallas_call | solution.py:291
  57.6 0.0 copy-start
  57.6 0.0 copy-start.1
  57.6 0.0 copy-start.2
  57.6 0.0 copy-start.3
  57.6 4.4 %all-to-all-start.1 = ((bf16[32,64,128]{2,1,0:T(8,128)(2,1)}), bf16[32,64,128]{2,1,0:T(8,128)(2,1)S(1)}, u32[]{:S(2)}, u32[]{:S(2)}) async-start(bf16[32,64,128]{2,1,0:T(8,128)(2,1)} %conv.1), calls=%async_computation.1 | async-start | bytes 1048576 | tf_op jit(solution)/shard_map/all_to_all | solution.py:268
  62.0 2.2 %collective-permute-start = (f32[16,1,128]{2,1,0:T(1,128)S(1)}, f32[16,1,128]{2,1,0:T(1,128)S(1)}, u32[]{:S(2)}, u32[]{:S(2)}) collective-permute-start(f32[16,1,128]{2,1,0:T(1,128)S(1)} %broadcast_select_fusion), channel_id=1, source_target_pairs={{0,24},{1,25},{2,26},{3,27},{4,28},{5,29},{6,30},{7,31},{8,16},{9,... | collective-permute-start | bytes 24584 | tf_op jit(solution)/shard_map/ppermute | solution.py:223
  64.3 5.4 %collective-permute-done = f32[16,1,128]{2,1,0:T(1,128)S(1)} collective-permute-done((f32[16,1,128]{2,1,0:T(1,128)S(1)}, f32[16,1,128]{2,1,0:T(1,128)S(1)}, u32[]{:S(2)}, u32[]{:S(2)}) %collective-permute-start) | collective-permute-done | bytes 8224 | tf_op jit(solution)/shard_map/ppermute | solution.py:223
  69.7 2.7 %collective-permute-start.1 = (f32[8,1,128]{2,1,0:T(1,128)S(1)}, f32[8,1,128]{2,1,0:T(1,128)S(1)}, u32[]{:S(2)}, u32[]{:S(2)}) collective-permute-start(f32[8,1,128]{2,1,0:T(1,128)S(1)} %broadcast_select_fusion.2), channel_id=1, source_target_pairs={{0,8},{1,9},{2,10},{3,11},{4,12},{5,13},{6,14},{7,15},{8,0},{9,1},... | collective-permute-start | bytes 12296 | tf_op jit(solution)/shard_map/ppermute | solution.py:223
  72.4 3.7 %collective-permute-done.1 = f32[8,1,128]{2,1,0:T(1,128)S(1)} collective-permute-done((f32[8,1,128]{2,1,0:T(1,128)S(1)}, f32[8,1,128]{2,1,0:T(1,128)S(1)}, u32[]{:S(2)}, u32[]{:S(2)}) %collective-permute-start.1) | collective-permute-done | bytes 4128 | tf_op jit(solution)/shard_map/ppermute | solution.py:223
  76.1 2.6 %collective-permute-start.2 = (f32[4,1,128]{2,1,0:T(1,128)S(1)}, f32[4,1,128]{2,1,0:T(1,128)S(1)}, u32[]{:S(2)}, u32[]{:S(2)}) collective-permute-start(f32[4,1,128]{2,1,0:T(1,128)S(1)} %broadcast_select_fusion.4), channel_id=1, source_target_pairs={{0,4},{1,5},{2,6},{3,7},{4,0},{5,1},{6,2},{7,3},{8,12},{9,13},{10,... | collective-permute-start | bytes 6152 | tf_op jit(solution)/shard_map/ppermute | solution.py:223
  78.7 2.9 %collective-permute-done.2 = f32[4,1,128]{2,1,0:T(1,128)S(1)} collective-permute-done((f32[4,1,128]{2,1,0:T(1,128)S(1)}, f32[4,1,128]{2,1,0:T(1,128)S(1)}, u32[]{:S(2)}, u32[]{:S(2)}) %collective-permute-start.2) | collective-permute-done | bytes 2080 | tf_op jit(solution)/shard_map/ppermute | solution.py:223
  81.6 4.6 %collective-permute-start.3 = (f32[2,1,128]{2,1,0:T(1,128)S(1)}, f32[2,1,128]{2,1,0:T(1,128)S(1)}, u32[]{:S(2)}, u32[]{:S(2)}) collective-permute-start(f32[2,1,128]{2,1,0:T(1,128)S(1)} %broadcast_select_fusion.6), channel_id=1, source_target_pairs={{0,2},{1,3},{2,0},{3,1},{4,6},{5,7},{6,4},{7,5},{8,10},{9,11},{10,... | collective-permute-start | bytes 3080 | tf_op jit(solution)/shard_map/ppermute | solution.py:223
  86.3 2.3 %collective-permute-done.3 = f32[2,1,128]{2,1,0:T(1,128)S(1)} collective-permute-done((f32[2,1,128]{2,1,0:T(1,128)S(1)}, f32[2,1,128]{2,1,0:T(1,128)S(1)}, u32[]{:S(2)}, u32[]{:S(2)}) %collective-permute-start.3) | collective-permute-done | bytes 1056 | tf_op jit(solution)/shard_map/ppermute | solution.py:223
  88.6 1.9 %collective-permute-start.4 = (f32[1,1,128]{2,1,0:T(1,128)S(1)}, f32[1,1,128]{2,1,0:T(1,128)S(1)}, u32[]{:S(2)}, u32[]{:S(2)}) collective-permute-start(f32[1,1,128]{2,1,0:T(1,128)S(1)} %get-tuple-element.23), channel_id=1, source_target_pairs={{0,1},{1,0},{2,3},{3,2},{4,5},{5,4},{6,7},{7,6},{8,9},{9,8},{10,11... | collective-permute-start | bytes 1544 | tf_op jit(solution)/shard_map/ppermute | solution.py:223
  90.5 1.1 %collective-permute-done.4.got_ref = f32[1,1,128]{2,1,0:T(1,128)S(1)} collective-permute-done((f32[1,1,128]{2,1,0:T(1,128)S(1)}, f32[1,1,128]{2,1,0:T(1,128)S(1)}, u32[]{:S(2)}, u32[]{:S(2)}) %collective-permute-start.4) | collective-permute-done | bytes 544 | tf_op jit(solution)/shard_map/ppermute | solution.py:223
  91.7 2.7 %all-to-all-done.1.in_ref = bf16[32,64,128]{2,1,0:T(8,128)(2,1)S(1)} async-done(((bf16[32,64,128]{2,1,0:T(8,128)(2,1)}), bf16[32,64,128]{2,1,0:T(8,128)(2,1)S(1)}, u32[]{:S(2)}, u32[]{:S(2)}) %all-to-all-start.1) | async-done | bytes 524320 | tf_op jit(solution)/shard_map/all_to_all | solution.py:268
  94.3 0.0 copy-done.1
  94.3 1.2 %close.1 = (bf16[128,1024]{1,0:T(8,128)(2,1)}, bf16[128,1024]{1,0:T(8,128)(2,1)}, bf16[128,1024]{1,0:T(8,128)(2,1)}, bf16[128,1024]{1,0:T(8,128)(2,1)}, f32[1,128]{1,0:T(1,128)}) custom-call(bf16[32,64,128]{2,1,0:T(8,128)(2,1)S(1)} %all-to-all-done.1.in_ref, bf16[128,1024]{1,0:T(8,128)(2,1)S(1)} %bitcast.20, bf16[128,1024]{1,0:T(8,128)(2,1)S(1)} %bitcast.22, ...), custom_call_target="tpu_custom_call" | custom-call | flops 524288 | bytes 2621440 | tf_op jit(solution)/shard_map/close/pallas_call | solution.py:309
  (13 shorter events, 0.1 us)
Async XLA Ops:
  2.1 51.5 %copy-start.4 = (bf16[1,4096]{1,0:T(2,128)(2,1)S(1)}, bf16[1,4096]{1,0:T(2,128)(2,1)}, u32[]{:S(2)}) copy-start(bf16[1,4096]{1,0:T(2,128)(2,1)} %f_ref.1) | copy-start | bytes 24580
  57.6 36.7 %copy-start = (bf16[1,128,1024]{2,1,0:T(8,128)(2,1)S(1)}, bf16[1,128,1024]{2,1,0:T(8,128)(2,1)}, u32[]{:S(2)}) copy-start(bf16[1,128,1024]{2,1,0:T(8,128)(2,1)} %param.6) | copy-start | bytes 786436
  57.6 36.7 %copy-start.1 = (bf16[1,128,1024]{2,1,0:T(8,128)(2,1)S(1)}, bf16[1,128,1024]{2,1,0:T(8,128)(2,1)}, u32[]{:S(2)}) copy-start(bf16[1,128,1024]{2,1,0:T(8,128)(2,1)} %param.7) | copy-start | bytes 786436
  57.6 36.7 %copy-start.2 = (bf16[1,128,1024]{2,1,0:T(8,128)(2,1)S(1)}, bf16[1,128,1024]{2,1,0:T(8,128)(2,1)}, u32[]{:S(2)}) copy-start(bf16[1,128,1024]{2,1,0:T(8,128)(2,1)} %param.5) | copy-start | bytes 786436
  57.6 36.7 %copy-start.3 = (bf16[1,128,1024]{2,1,0:T(8,128)(2,1)S(1)}, bf16[1,128,1024]{2,1,0:T(8,128)(2,1)}, u32[]{:S(2)}) copy-start(bf16[1,128,1024]{2,1,0:T(8,128)(2,1)} %param.8) | copy-start | bytes 786436
  57.6 36.7 %all-to-all-start.1 = ((bf16[32,64,128]{2,1,0:T(8,128)(2,1)}), bf16[32,64,128]{2,1,0:T(8,128)(2,1)S(1)}, u32[]{:S(2)}, u32[]{:S(2)}) async-start(bf16[32,64,128]{2,1,0:T(8,128)(2,1)} %conv.1), calls=%async_computation.1 | async-start | bytes 1048576 | tf_op jit(solution)/shard_map/all_to_all | solution.py:268
  62.0 7.7 %collective-permute-start = (f32[16,1,128]{2,1,0:T(1,128)S(1)}, f32[16,1,128]{2,1,0:T(1,128)S(1)}, u32[]{:S(2)}, u32[]{:S(2)}) collective-permute-start(f32[16,1,128]{2,1,0:T(1,128)S(1)} %broadcast_select_fusion), channel_id=1, source_target_pairs={{0,24},{1,25},{2,26},{3,27},{4,28},{5,29},{6,30},{7,31},{8,16},{9,... | collective-permute-start | bytes 24584 | tf_op jit(solution)/shard_map/ppermute | solution.py:223
  69.7 6.4 %collective-permute-start.1 = (f32[8,1,128]{2,1,0:T(1,128)S(1)}, f32[8,1,128]{2,1,0:T(1,128)S(1)}, u32[]{:S(2)}, u32[]{:S(2)}) collective-permute-start(f32[8,1,128]{2,1,0:T(1,128)S(1)} %broadcast_select_fusion.2), channel_id=1, source_target_pairs={{0,8},{1,9},{2,10},{3,11},{4,12},{5,13},{6,14},{7,15},{8,0},{9,1},... | collective-permute-start | bytes 12296 | tf_op jit(solution)/shard_map/ppermute | solution.py:223
  76.1 5.5 %collective-permute-start.2 = (f32[4,1,128]{2,1,0:T(1,128)S(1)}, f32[4,1,128]{2,1,0:T(1,128)S(1)}, u32[]{:S(2)}, u32[]{:S(2)}) collective-permute-start(f32[4,1,128]{2,1,0:T(1,128)S(1)} %broadcast_select_fusion.4), channel_id=1, source_target_pairs={{0,4},{1,5},{2,6},{3,7},{4,0},{5,1},{6,2},{7,3},{8,12},{9,13},{10,... | collective-permute-start | bytes 6152 | tf_op jit(solution)/shard_map/ppermute | solution.py:223
  81.6 7.0 %collective-permute-start.3 = (f32[2,1,128]{2,1,0:T(1,128)S(1)}, f32[2,1,128]{2,1,0:T(1,128)S(1)}, u32[]{:S(2)}, u32[]{:S(2)}) collective-permute-start(f32[2,1,128]{2,1,0:T(1,128)S(1)} %broadcast_select_fusion.6), channel_id=1, source_target_pairs={{0,2},{1,3},{2,0},{3,1},{4,6},{5,7},{6,4},{7,5},{8,10},{9,11},{10,... | collective-permute-start | bytes 3080 | tf_op jit(solution)/shard_map/ppermute | solution.py:223
  88.6 3.1 %collective-permute-start.4 = (f32[1,1,128]{2,1,0:T(1,128)S(1)}, f32[1,1,128]{2,1,0:T(1,128)S(1)}, u32[]{:S(2)}, u32[]{:S(2)}) collective-permute-start(f32[1,1,128]{2,1,0:T(1,128)S(1)} %get-tuple-element.23), channel_id=1, source_target_pairs={{0,1},{1,0},{2,3},{3,2},{4,5},{5,4},{6,7},{7,6},{8,9},{9,8},{10,11... | collective-permute-start | bytes 1544 | tf_op jit(solution)/shard_map/ppermute | solution.py:223

commit v7 on v6

--- a/solution.py
+++ b/solution.py
@@ -18,6 +18,7 @@
 ANY = pl.BlockSpec(memory_space=pl.ANY)
 DMA = pltpu.SemaphoreType.DMA
 PARTS = 4
+LOADS = 2
 
 
 def call(kernel, out_shape, flops, moved, outs, limit=16, **kw):
@@ -33,10 +34,10 @@
 
 def gate_kernel(k_ref, v_ref, q_ref, g_ref, out_ref, wide_ref, in_sem):
     groups, _, pos = out_ref.shape
-    step = groups // PARTS
+    step = groups // LOADS
     span = step * CPG
     loads = []
-    for part in range(PARTS):
+    for part in range(LOADS):
         at = pl.ds(part * span, span)
         row = [
             pltpu.make_async_copy(ref.at[:, at], wide_ref.at[i, :, at], in_sem.at[part, i])
@@ -45,14 +46,14 @@
         for copy in row:
             copy.start()
         loads.append(row)
-    for part in range(PARTS):
+    for part in range(LOADS):
         for copy in loads[part]:
             copy.wait()
         at = slice(part * span, (part + 1) * span)
         mine = slice(part * step, (part + 1) * step)
         for h in range(2):
-            one = wide_ref[2 * h, :, at].astype(F32) * wide_ref[2 * h + 1, :, at].astype(F32)
-            rows = one.astype(BF16).T.reshape(step, CPG, pos)
+            one = wide_ref[2 * h, :, at] * wide_ref[2 * h + 1, :, at]
+            rows = one.T.reshape(step, CPG, pos)
             out_ref[mine, h * CPG : (h + 1) * CPG, :] = rows
 
 
@@ -197,10 +198,10 @@
         at = slice(part * span, (part + 1) * span)
         for h, gates, outs in ((0, (q_ref, g_ref), (out_ref, gq_ref)), (1, (v_ref, k_ref), (gk_ref, gv_ref))):
             rows = in_ref[part * step : (part + 1) * step, h * CPG : (h + 1) * CPG, :]
-            wide = rows.reshape(span, pos).T.astype(F32)
+            wide = rows.reshape(span, pos).T
             for j in range(2):
                 i = 2 * h + j
-                held_ref[i, :, at] = (gates[j][:, at].astype(F32) * wide).astype(BF16)
+                held_ref[i, :, at] = gates[j][:, at] * wide
                 into = outs[j].at[:, pl.ds(part * span, span)]
                 copy = pltpu.make_async_copy(
                     held_ref.at[i, :, pl.ds(part * span, span)], into, sem.at[part, i]
@@ -243,7 +244,7 @@
         3 * size,
         VMEM,
         in_specs=[ANY] * 4,
-        scratch_shapes=[pltpu.VMEM((4, pos, channels), BF16), DMA((PARTS, 4))],
+        scratch_shapes=[pltpu.VMEM((4, pos, channels), BF16), DMA((LOADS, 4))],
         name="gate",
     )(*[pltpu.with_memory_space_constraint(a, pltpu.HBM) for a in flat])
     owned = lax.all_to_all(sent, "ctx", split_axis=0, concat_axis=0, tiled=True)

time: 96 us -> 96 us (level)
  the two profiles are of different devices: /device:TPU:96 before, /device:TPU:112 now
where the time goes in v7:
time: 96 us; the launch traced here: 95.5 us
  blocking collectives  51.5 us (54%)
  starting transfers between devices  19.4 us (20%)
  waiting for transfers between devices  17.1 us (18%)
  Pallas kernels  6.58 us (7%)
    all_to_all x1, blocking collectives, step(): owned = lax.all_to_all(sent, 'ctx', split_axis=0, concat_axis=0, tiled=True)  51.5 us
    ppermute x5, starting transfers between devices, halve(): got = lax.ppermute(away, 'dp', [(i, i ^ mask) for i in range(replicas)])  15.1 us
    ppermute x5, waiting for transfers between devices, halve(): got = lax.ppermute(away, 'dp', [(i, i ^ mask) for i in range(replicas)])  14.4 us
    all_to_all x1, starting transfers between devices, step(): lax.all_to_all(result, 'ctx', split_axis=0, concat_axis=0, tiled=True)  4.35 us
    all_to_all x1, waiting for transfers between devices, step(): lax.all_to_all(result, 'ctx', split_axis=0, concat_axis=0, tiled=True)  2.67 us
    pallas_call x1, Pallas kernels, step(): call(conv_kernel, held, 2 * work, 2 * size + BLK * length * 2, ANY, in_sp...  2.48 us
  transfers between devices with their start and end apart: 6, of which 6 were waited for; matrix products, arithmetic and copies ran while one was open for 0% of the time, Pallas kernels for 0%

profile of v7, /device:TPU:112, one launch (start us, length us, event | category | flops | bytes accessed | tf_op | source)
XLA Modules:
  0.0 95.5 jit_solution(7223211318069345978)
XLA Ops:
  0.6 1.5 %gate.1 = bf16[32,64,128]{2,1,0:T(8,128)(2,1)S(1)} custom-call(bf16[128,1024]{1,0:T(8,128)(2,1)} %bitcast.19, bf16[128,1024]{1,0:T(8,128)(2,1)} %bitcast.21, bf16[128,1024]{1,0:T(8,128)(2,1)} %bitcast.23, bf16[128,1024]{1,0:T(8,128)(2,1)} %bitcast.25), custom_call_target="tpu_custom_call" | custom-call | flops 262144 | bytes 1572864 | tf_op jit(solution)/shard_map/gate/pallas_call | solution.py:240
  2.1 0.0 copy-start.4
  2.1 51.5 %all_to_all.10.in_ref.refs_0_ = bf16[32,64,128]{2,1,0:T(8,128)(2,1)S(1)} all-to-all(bf16[32,64,128]{2,1,0:T(8,128)(2,1)S(1)} %gate.1), channel_id=1, replica_groups=mesh['ctx'=32,'dp'=32] {'ctx'}, dimensions={0} | all-to-all | bytes 1048576 | tf_op jit(solution)/shard_map/all_to_all | solution.py:250
  53.6 0.0 copy-done.4
  53.6 2.5 %conv.1 = bf16[32,64,128]{2,1,0:T(8,128)(2,1)} custom-call(bf16[32,64,128]{2,1,0:T(8,128)(2,1)S(1)} %all_to_all.10.in_ref.refs_0_, bf16[1,4096]{1,0:T(2,128)(2,1)S(1)} %copy-done.4), custom_call_target="tpu_custom_call" | custom-call | flops 2147483648 | bytes 3145728 | tf_op jit(solution)/shard_map/conv/pallas_call | solution.py:252
  56.1 1.4 %lags.1 = (f32[32,1,128]{2,1,0:T(1,128)S(1)}, s32[1,128]{1,0:T(1,128)S(1)}) custom-call(bf16[32,64,128]{2,1,0:T(8,128)(2,1)S(1)} %all_to_all.10.in_ref.refs_0_), custom_call_target="tpu_custom_call" | custom-call | flops 1073741824 | bytes 8912896 | tf_op jit(solution)/shard_map/lags/pallas_call | solution.py:292
  57.6 0.0 copy-start
  57.6 0.0 copy-start.1
  57.6 0.0 copy-start.2
  57.6 0.0 copy-start.3
  57.6 4.4 %all-to-all-start.1 = ((bf16[32,64,128]{2,1,0:T(8,128)(2,1)}), bf16[32,64,128]{2,1,0:T(8,128)(2,1)S(1)}, u32[]{:S(2)}, u32[]{:S(2)}) async-start(bf16[32,64,128]{2,1,0:T(8,128)(2,1)} %conv.1), calls=%async_computation.1 | async-start | bytes 1048576 | tf_op jit(solution)/shard_map/all_to_all | solution.py:269
  62.0 1.9 %collective-permute-start = (f32[16,1,128]{2,1,0:T(1,128)S(1)}, f32[16,1,128]{2,1,0:T(1,128)S(1)}, u32[]{:S(2)}, u32[]{:S(2)}) collective-permute-start(f32[16,1,128]{2,1,0:T(1,128)S(1)} %broadcast_select_fusion), channel_id=1, source_target_pairs={{0,24},{1,25},{2,26},{3,27},{4,28},{5,29},{6,30},{7,31},{8,16},{9,... | collective-permute-start | bytes 24584 | tf_op jit(solution)/shard_map/ppermute | solution.py:224
  63.9 5.7 %collective-permute-done = f32[16,1,128]{2,1,0:T(1,128)S(1)} collective-permute-done((f32[16,1,128]{2,1,0:T(1,128)S(1)}, f32[16,1,128]{2,1,0:T(1,128)S(1)}, u32[]{:S(2)}, u32[]{:S(2)}) %collective-permute-start) | collective-permute-done | bytes 8224 | tf_op jit(solution)/shard_map/ppermute | solution.py:224
  69.7 4.0 %collective-permute-start.1 = (f32[8,1,128]{2,1,0:T(1,128)S(1)}, f32[8,1,128]{2,1,0:T(1,128)S(1)}, u32[]{:S(2)}, u32[]{:S(2)}) collective-permute-start(f32[8,1,128]{2,1,0:T(1,128)S(1)} %broadcast_select_fusion.2), channel_id=1, source_target_pairs={{0,8},{1,9},{2,10},{3,11},{4,12},{5,13},{6,14},{7,15},{8,0},{9,1},... | collective-permute-start | bytes 12296 | tf_op jit(solution)/shard_map/ppermute | solution.py:224
  73.7 2.4 %collective-permute-done.1 = f32[8,1,128]{2,1,0:T(1,128)S(1)} collective-permute-done((f32[8,1,128]{2,1,0:T(1,128)S(1)}, f32[8,1,128]{2,1,0:T(1,128)S(1)}, u32[]{:S(2)}, u32[]{:S(2)}) %collective-permute-start.1) | collective-permute-done | bytes 4128 | tf_op jit(solution)/shard_map/ppermute | solution.py:224
  76.1 2.6 %collective-permute-start.2 = (f32[4,1,128]{2,1,0:T(1,128)S(1)}, f32[4,1,128]{2,1,0:T(1,128)S(1)}, u32[]{:S(2)}, u32[]{:S(2)}) collective-permute-start(f32[4,1,128]{2,1,0:T(1,128)S(1)} %broadcast_select_fusion.4), channel_id=1, source_target_pairs={{0,4},{1,5},{2,6},{3,7},{4,0},{5,1},{6,2},{7,3},{8,12},{9,13},{10,... | collective-permute-start | bytes 6152 | tf_op jit(solution)/shard_map/ppermute | solution.py:224
  78.7 2.9 %collective-permute-done.2 = f32[4,1,128]{2,1,0:T(1,128)S(1)} collective-permute-done((f32[4,1,128]{2,1,0:T(1,128)S(1)}, f32[4,1,128]{2,1,0:T(1,128)S(1)}, u32[]{:S(2)}, u32[]{:S(2)}) %collective-permute-start.2) | collective-permute-done | bytes 2080 | tf_op jit(solution)/shard_map/ppermute | solution.py:224
  81.6 4.6 %collective-permute-start.3 = (f32[2,1,128]{2,1,0:T(1,128)S(1)}, f32[2,1,128]{2,1,0:T(1,128)S(1)}, u32[]{:S(2)}, u32[]{:S(2)}) collective-permute-start(f32[2,1,128]{2,1,0:T(1,128)S(1)} %broadcast_select_fusion.6), channel_id=1, source_target_pairs={{0,2},{1,3},{2,0},{3,1},{4,6},{5,7},{6,4},{7,5},{8,10},{9,11},{10,... | collective-permute-start | bytes 3080 | tf_op jit(solution)/shard_map/ppermute | solution.py:224
  86.2 2.3 %collective-permute-done.3 = f32[2,1,128]{2,1,0:T(1,128)S(1)} collective-permute-done((f32[2,1,128]{2,1,0:T(1,128)S(1)}, f32[2,1,128]{2,1,0:T(1,128)S(1)}, u32[]{:S(2)}, u32[]{:S(2)}) %collective-permute-start.3) | collective-permute-done | bytes 1056 | tf_op jit(solution)/shard_map/ppermute | solution.py:224
  88.6 1.9 %collective-permute-start.4 = (f32[1,1,128]{2,1,0:T(1,128)S(1)}, f32[1,1,128]{2,1,0:T(1,128)S(1)}, u32[]{:S(2)}, u32[]{:S(2)}) collective-permute-start(f32[1,1,128]{2,1,0:T(1,128)S(1)} %get-tuple-element.23), channel_id=1, source_target_pairs={{0,1},{1,0},{2,3},{3,2},{4,5},{5,4},{6,7},{7,6},{8,9},{9,8},{10,11... | collective-permute-start | bytes 1544 | tf_op jit(solution)/shard_map/ppermute | solution.py:224
  90.5 1.1 %collective-permute-done.4.got_ref = f32[1,1,128]{2,1,0:T(1,128)S(1)} collective-permute-done((f32[1,1,128]{2,1,0:T(1,128)S(1)}, f32[1,1,128]{2,1,0:T(1,128)S(1)}, u32[]{:S(2)}, u32[]{:S(2)}) %collective-permute-start.4) | collective-permute-done | bytes 544 | tf_op jit(solution)/shard_map/ppermute | solution.py:224
  91.6 2.7 %all-to-all-done.1.in_ref = bf16[32,64,128]{2,1,0:T(8,128)(2,1)S(1)} async-done(((bf16[32,64,128]{2,1,0:T(8,128)(2,1)}), bf16[32,64,128]{2,1,0:T(8,128)(2,1)S(1)}, u32[]{:S(2)}, u32[]{:S(2)}) %all-to-all-start.1) | async-done | bytes 524320 | tf_op jit(solution)/shard_map/all_to_all | solution.py:269
  94.3 0.0 copy-done.3
  94.3 1.2 %close.1 = (bf16[128,1024]{1,0:T(8,128)(2,1)}, bf16[128,1024]{1,0:T(8,128)(2,1)}, bf16[128,1024]{1,0:T(8,128)(2,1)}, bf16[128,1024]{1,0:T(8,128)(2,1)}, f32[1,128]{1,0:T(1,128)}) custom-call(bf16[32,64,128]{2,1,0:T(8,128)(2,1)S(1)} %all-to-all-done.1.in_ref, bf16[128,1024]{1,0:T(8,128)(2,1)S(1)} %bitcast.20, bf16[128,1024]{1,0:T(8,128)(2,1)S(1)} %bitcast.22, ...), custom_call_target="tpu_custom_call" | custom-call | flops 524288 | bytes 2621440 | tf_op jit(solution)/shard_map/close/pallas_call | solution.py:310
  (13 shorter events, 0.1 us)
Async XLA Ops:
  2.1 51.5 %copy-start.4 = (bf16[1,4096]{1,0:T(2,128)(2,1)S(1)}, bf16[1,4096]{1,0:T(2,128)(2,1)}, u32[]{:S(2)}) copy-start(bf16[1,4096]{1,0:T(2,128)(2,1)} %f_ref.1) | copy-start | bytes 24580
  57.6 36.7 %copy-start = (bf16[1,128,1024]{2,1,0:T(8,128)(2,1)S(1)}, bf16[1,128,1024]{2,1,0:T(8,128)(2,1)}, u32[]{:S(2)}) copy-start(bf16[1,128,1024]{2,1,0:T(8,128)(2,1)} %param.6) | copy-start | bytes 786436
  57.6 36.7 %copy-start.1 = (bf16[1,128,1024]{2,1,0:T(8,128)(2,1)S(1)}, bf16[1,128,1024]{2,1,0:T(8,128)(2,1)}, u32[]{:S(2)}) copy-start(bf16[1,128,1024]{2,1,0:T(8,128)(2,1)} %param.7) | copy-start | bytes 786436
  57.6 36.7 %copy-start.2 = (bf16[1,128,1024]{2,1,0:T(8,128)(2,1)S(1)}, bf16[1,128,1024]{2,1,0:T(8,128)(2,1)}, u32[]{:S(2)}) copy-start(bf16[1,128,1024]{2,1,0:T(8,128)(2,1)} %param.5) | copy-start | bytes 786436
  57.6 36.7 %copy-start.3 = (bf16[1,128,1024]{2,1,0:T(8,128)(2,1)S(1)}, bf16[1,128,1024]{2,1,0:T(8,128)(2,1)}, u32[]{:S(2)}) copy-start(bf16[1,128,1024]{2,1,0:T(8,128)(2,1)} %param.8) | copy-start | bytes 786436
  57.6 36.7 %all-to-all-start.1 = ((bf16[32,64,128]{2,1,0:T(8,128)(2,1)}), bf16[32,64,128]{2,1,0:T(8,128)(2,1)S(1)}, u32[]{:S(2)}, u32[]{:S(2)}) async-start(bf16[32,64,128]{2,1,0:T(8,128)(2,1)} %conv.1), calls=%async_computation.1 | async-start | bytes 1048576 | tf_op jit(solution)/shard_map/all_to_all | solution.py:269
  62.0 7.7 %collective-permute-start = (f32[16,1,128]{2,1,0:T(1,128)S(1)}, f32[16,1,128]{2,1,0:T(1,128)S(1)}, u32[]{:S(2)}, u32[]{:S(2)}) collective-permute-start(f32[16,1,128]{2,1,0:T(1,128)S(1)} %broadcast_select_fusion), channel_id=1, source_target_pairs={{0,24},{1,25},{2,26},{3,27},{4,28},{5,29},{6,30},{7,31},{8,16},{9,... | collective-permute-start | bytes 24584 | tf_op jit(solution)/shard_map/ppermute | solution.py:224
  69.7 6.4 %collective-permute-start.1 = (f32[8,1,128]{2,1,0:T(1,128)S(1)}, f32[8,1,128]{2,1,0:T(1,128)S(1)}, u32[]{:S(2)}, u32[]{:S(2)}) collective-permute-start(f32[8,1,128]{2,1,0:T(1,128)S(1)} %broadcast_select_fusion.2), channel_id=1, source_target_pairs={{0,8},{1,9},{2,10},{3,11},{4,12},{5,13},{6,14},{7,15},{8,0},{9,1},... | collective-permute-start | bytes 12296 | tf_op jit(solution)/shard_map/ppermute | solution.py:224
  76.1 5.5 %collective-permute-start.2 = (f32[4,1,128]{2,1,0:T(1,128)S(1)}, f32[4,1,128]{2,1,0:T(1,128)S(1)}, u32[]{:S(2)}, u32[]{:S(2)}) collective-permute-start(f32[4,1,128]{2,1,0:T(1,128)S(1)} %broadcast_select_fusion.4), channel_id=1, source_target_pairs={{0,4},{1,5},{2,6},{3,7},{4,0},{5,1},{6,2},{7,3},{8,12},{9,13},{10,... | collective-permute-start | bytes 6152 | tf_op jit(solution)/shard_map/ppermute | solution.py:224
  81.6 7.0 %collective-permute-start.3 = (f32[2,1,128]{2,1,0:T(1,128)S(1)}, f32[2,1,128]{2,1,0:T(1,128)S(1)}, u32[]{:S(2)}, u32[]{:S(2)}) collective-permute-start(f32[2,1,128]{2,1,0:T(1,128)S(1)} %broadcast_select_fusion.6), channel_id=1, source_target_pairs={{0,2},{1,3},{2,0},{3,1},{4,6},{5,7},{6,4},{7,5},{8,10},{9,11},{10,... | collective-permute-start | bytes 3080 | tf_op jit(solution)/shard_map/ppermute | solution.py:224
  88.6 3.1 %collective-permute-start.4 = (f32[1,1,128]{2,1,0:T(1,128)S(1)}, f32[1,1,128]{2,1,0:T(1,128)S(1)}, u32[]{:S(2)}, u32[]{:S(2)}) collective-permute-start(f32[1,1,128]{2,1,0:T(1,128)S(1)} %get-tuple-element.23), channel_id=1, source_target_pairs={{0,1},{1,0},{2,3},{3,2},{4,5},{5,4},{6,7},{7,6},{8,9},{9,8},{10,11... | collective-permute-start | bytes 1544 | tf_op jit(solution)/shard_map/ppermute | solution.py:224
